TPU v7x, 128 devices: a whole 4x4x4 slice. The times are simulated.
128 devices in a mesh: pipe: 4 (over y), dp: 4 (over z_hi, core), tensor: 8 (over z_lo, x).
Axes of the slice: x: 4, y: 4, z: 4 (z_hi: 2, z_lo: 2; z = z_hi * 2 + z_lo), core: 2. Of those that a mesh axis runs over, the one named last changes fastest.
Arguments:
- output_gradient: bfloat16 [16, 128, 8192], P('dp', None, 'tensor'), may hold values from -6 to 6
- acts: bfloat16 [16, 4, 128, 8192], P('dp', 'pipe', None, 'tensor'), may hold values from -6 to 6
- weights: bfloat16 [4, 8192, 8192], P('pipe', 'tensor'), may hold values from -0.0625 to 0.0625
- adapter_down_factors: bfloat16 [4, 8192, 128], P('pipe', 'tensor'), may hold values from -0.0625 to 0.0625
- adapter_up_factors: bfloat16 [4, 128, 8192], P('pipe'), may hold values from -0.0625 to 0.0625
- feature_sign_bits: int32 [8192, 64], replicated, may hold values from 0 to 1
- rank_sign_bits: int32 [128, 128], replicated, may hold values from 0 to 1
- lengths: int32 [16], P('dp'), may hold values from 32 to 128, as said below
Outputs:
- features: float32 [16, 4, 8192], P('dp', 'pipe', 'tensor')
Inputs may be any that keep to these rules, and one draw needn't show every extreme that they name: `lengths`: the first example has exactly 128 real tokens.
All inputs are finite; a program needn't handle non-finite values.
Results may differ from a plain program's by a relative error of at most 0.0065.
Values may be sent and summed in bfloat16 or wider, within the bound.
A program may use at most 128 MiB of HBM per device.

v0:
```python
import math

import jax
import jax.numpy as jnp
from jax import lax
from jax.sharding import PartitionSpec as P

ADAPTER_SCALE = 2.0
F32 = jnp.float32
BF16 = jnp.bfloat16


def tn(left, right, **kw):
    return lax.dot_general(left, right, (((0,), (0,)), ((), ())), preferred_element_type=F32, **kw)


def per_device(g, acts, weights, down, up, wide_bits, rank_bits, lengths):
    sections = lax.axis_size("pipe")
    s = lax.axis_index("pipe")
    parts = lax.axis_size("tensor")
    t = lax.axis_index("tensor")
    groups = lax.axis_size("dp")
    d = lax.axis_index("dp")
    count, seq, local = g.shape
    width = local * parts
    rank = up.shape[1]
    proj = wide_bits.shape[1]
    sub = local // groups

    w = weights[0].reshape(local, parts, groups, sub)
    w = lax.dynamic_index_in_dim(w, d, 2, False).reshape(local, parts * sub)
    b_sel = up[0].reshape(rank, parts, groups, sub)
    b_sel = lax.dynamic_index_in_dim(b_sel, d, 2, False).reshape(rank, parts * sub)
    a = down[0]
    b_loc = lax.dynamic_slice_in_dim(up[0], t * local, local, 1)
    wide = lax.dynamic_slice_in_dim(wide_bits, t * local, local, 0)
    wide = (2 * wide - 1).astype(BF16)
    low = (2 * rank_bits - 1).astype(BF16)
    qa, qb = low[:, :proj], low[:, proj:]

    bq = tn(b_loc, qa).astype(BF16)
    here = jnp.concatenate([bq, wide], axis=1)
    mine = jnp.where(s == sections - 1, here, jnp.zeros_like(here))
    up_one = [(i, i + 1) for i in range(sections - 1)]
    right = jnp.concatenate([lax.ppermute(bq, "pipe", up_one), wide], axis=1)
    for k in range(1, sections):
        small = tn(a, right).astype(BF16)
        part = tn(w, right) + ADAPTER_SCALE * tn(b_sel, small)
        whole = lax.psum_scatter(part, "tensor", scatter_dimension=0, tiled=True).astype(BF16)
        block = lax.all_gather(whole, "dp", axis=0, tiled=True)
        mine = mine + lax.ppermute(block, "pipe", [(sections - 1, sections - 1 - k)])
        if k + 1 < sections:
            right = lax.ppermute(block, "pipe", up_one)

    tokens = count * seq
    y_part = jnp.dot(g.reshape(tokens, local), mine, preferred_element_type=F32)
    x = acts[:, 0].reshape(tokens, local)
    xp = jnp.dot(x, wide, preferred_element_type=F32)
    xa = jnp.dot(x, a, preferred_element_type=F32)
    xb = jnp.dot(xa, qb.astype(F32), precision=lax.Precision.HIGHEST, preferred_element_type=F32)
    x_part = jnp.concatenate([xp, xb], axis=1)
    y = lax.psum_scatter(y_part, "tensor", scatter_dimension=0, tiled=True)
    xs = lax.psum_scatter(x_part, "tensor", scatter_dimension=0, tiled=True)
    per = tokens // parts
    index = t * per + jnp.arange(per)
    keep = (index % seq < lengths[index // seq]).astype(F32)[:, None]
    scale = ADAPTER_SCALE / math.sqrt(seq) / math.sqrt(width) / math.sqrt(rank)
    xs = xs * keep * scale
    hi = lax.Precision.HIGHEST
    left = tn(xs[:, :proj], y[:, :proj], precision=hi)
    rite = tn(xs[:, proj:], y[:, proj:], precision=hi)
    full = jnp.concatenate([left.reshape(-1), rite.reshape(-1)]).reshape(parts, -1)
    got = lax.all_to_all(full, "tensor", 0, 0, tiled=True)
    return got.reshape(count, parts // count, -1).sum(1)[:, None, :]


def solution(mesh):
    placed = (
        P("dp", None, "tensor"),
        P("dp", "pipe", None, "tensor"),
        P("pipe", "tensor", None),
        P("pipe", "tensor", None),
        P("pipe", None, None),
        P(),
        P(),
        P("dp"),
    )
    return jax.shard_map(
        per_device, mesh=mesh, in_specs=placed, out_specs=P("dp", "pipe", "tensor"), check_vma=False
    )
```

profile of v0, /device:TPU:0, one launch (start us, length us, event | category | flops | bytes accessed | tf_op | source)
XLA Modules:
  0.0 322.7 jit_solution(694221434962773035)
XLA Ops:
  6.5 0.9 add_convert_fusion.1
  7.5 1.8 convolution_convert_fusion
  9.3 4.2 %collective-permute-start = (bf16[1024,64]{0,1:T(8,128)(2,1)}, bf16[1024,64]{0,1:T(8,128)(2,1)}, u32[]{:S(2)}, u32[]{:S(2)}) collective-permute-start(bf16[1024,64]{0,1:T(8,128)(2,1)} %convolution_convert_fusion), channel_id=1, source_target_pairs={{0,32},{32,64},{64,96},{1,33},{33,65},{65,97},{2,34},{34,66},{66,9... | collective-permute-start | bytes 393224 | tf_op jit(solution)/shard_map/ppermute | solution.py:45
  13.6 22.4 %copy.25 = bf16[1,1024,8192]{1,2,0:T(8,128)(2,1)} copy(bf16[1,1024,8192]{2,1,0:T(8,128)(2,1)} %param.10) | data formatting | bytes 33554432 | tf_op args[2]
  35.9 4.7 %constant_dynamic-slice_fusion.1 = bf16[1024,8,1,256]{0,3,2,1:T(8,128)(2,1)} fusion(bf16[1024,8,4,256]{0,3,2,1:T(8,128)(2,1)} %bitcast.55, s32[]{:T(128)S(6)} %select_n.57), kind=kLoop, calls=%fused_computation.55 | loop fusion | bytes 8388612 | tf_op jit(solution)/shard_map/jit(dynamic_index_in_dim)/dynamic_slice | solution.py:31
  40.7 1.0 add_convert_fusion
  41.7 2.5 copy.26
  44.2 1.1 constant_dynamic-slice_fusion
  45.3 1.4 convolution_multiply_fusion.2
  46.6 4.7 %convolution_add_fusion.2 = f32[2048,128]{0,1:T(8,128)} fusion(f32[2048,128]{0,1:T(8,128)S(1)} %convolution_multiply_fusion.2, bf16[1024,2048]{0,1:T(8,128)(2,1)} %bitcast.52, bf16[1024,64]{0,1:T(8,128)(2,1)S(1)} %add_convert_fusion, bf16[1024,64]{0,1:T(8,128)(2,1)} %collective-permute-done), kind=kOutput, calls=%fused_computation.5 | convolution fusion | flops 537657344 | bytes 6553600 | tf_op jit(solution)/shard_map/dot_general | solution.py:14
  51.4 41.1 %reduce-scatter.10.cloned.1.call-done = f32[256,128]{0,1:T(8,128)} async-done(((f32[2048,128]{0,1:T(8,128)}), f32[256,128]{0,1:T(8,128)}) %reduce-scatter.10.cloned.1.call-update) | async-done | bytes 131088 | tf_op jit(solution)/shard_map/reduce_scatter | solution.py:49
  92.5 0.9 convert_element_type.43
  93.4 7.7 %all_gather.9 = bf16[1024,128]{0,1:T(8,128)(2,1)} all-gather(bf16[256,128]{0,1:T(8,128)(2,1)S(1)} %convert_element_type.43), channel_id=1, replica_groups=mesh['pipe'=4,'dp'=4,'tensor'=8] {'dp'}, dimensions={0}, use_global_device_ids=true | all-gather | bytes 327680 | tf_op jit(solution)/shard_map/all_gather | solution.py:50
  101.1 3.4 %collective-permute-start.2 = (bf16[1024,128]{0,1:T(8,128)(2,1)}, bf16[1024,128]{0,1:T(8,128)(2,1)S(1)}, u32[]{:S(2)}, u32[]{:S(2)}) collective-permute-start(bf16[1024,128]{0,1:T(8,128)(2,1)} %all_gather.9), channel_id=1, source_target_pairs={{0,32},{32,64},{64,96},{1,33},{33,65},{65,97},{2,34},{34,66},{66,9... | collective-permute-start | bytes 786440 | tf_op jit(solution)/shard_map/ppermute | solution.py:53
  104.5 6.4 %collective-permute-done.2 = bf16[1024,128]{0,1:T(8,128)(2,1)S(1)} collective-permute-done((bf16[1024,128]{0,1:T(8,128)(2,1)}, bf16[1024,128]{0,1:T(8,128)(2,1)S(1)}, u32[]{:S(2)}, u32[]{:S(2)}) %collective-permute-start.2) | collective-permute-done | bytes 262176 | tf_op jit(solution)/shard_map/ppermute | solution.py:53
  111.3 4.7 %convolution_add_fusion.1 = f32[2048,128]{0,1:T(8,128)} fusion(f32[2048,128]{0,1:T(8,128)S(1)} %convolution_multiply_fusion.1, bf16[1024,2048]{0,1:T(8,128)(2,1)} %bitcast.53, bf16[1024,128]{0,1:T(8,128)(2,1)S(1)} %collective-permute-done.2), kind=kOutput, calls=%fused_computation.3 | convolution fusion | flops 537133056 | bytes 6553600 | tf_op jit(solution)/shard_map/dot_general | solution.py:14
  116.0 39.3 %reduce-scatter.12.cloned.1.call-done = f32[256,128]{0,1:T(8,128)} async-done(((f32[2048,128]{0,1:T(8,128)}), f32[256,128]{0,1:T(8,128)}) %reduce-scatter.12.cloned.1.call-update) | async-done | bytes 131088 | tf_op jit(solution)/shard_map/reduce_scatter | solution.py:49
  156.2 7.3 %all_gather.10 = bf16[1024,128]{0,1:T(8,128)(2,1)S(1)} all-gather(bf16[256,128]{0,1:T(8,128)(2,1)S(1)} %convert_element_type.45), channel_id=1, replica_groups=mesh['pipe'=4,'dp'=4,'tensor'=8] {'dp'}, dimensions={0}, use_global_device_ids=true | all-gather | bytes 327680 | tf_op jit(solution)/shard_map/all_gather | solution.py:50
  163.5 3.4 %collective-permute-start.4 = (bf16[1024,128]{0,1:T(8,128)(2,1)S(1)}, bf16[1024,128]{0,1:T(8,128)(2,1)S(1)}, u32[]{:S(2)}, u32[]{:S(2)}) collective-permute-start(bf16[1024,128]{0,1:T(8,128)(2,1)S(1)} %all_gather.10), channel_id=1, source_target_pairs={{0,32},{32,64},{64,96},{1,33},{33,65},{65,97},{2,34},{34,66},{66,9... | collective-permute-start | bytes 786440 | tf_op jit(solution)/shard_map/ppermute | solution.py:53
  167.0 6.0 %collective-permute-done.4 = bf16[1024,128]{0,1:T(8,128)(2,1)S(1)} collective-permute-done((bf16[1024,128]{0,1:T(8,128)(2,1)S(1)}, bf16[1024,128]{0,1:T(8,128)(2,1)S(1)}, u32[]{:S(2)}, u32[]{:S(2)}) %collective-permute-start.4) | collective-permute-done | bytes 262176 | tf_op jit(solution)/shard_map/ppermute | solution.py:53
  173.5 4.7 %convolution_add_fusion = f32[2048,128]{0,1:T(8,128)} fusion(f32[2048,128]{0,1:T(8,128)S(1)} %convolution_multiply_fusion, bf16[1024,2048]{0,1:T(8,128)(2,1)} %bitcast.54, bf16[1024,128]{0,1:T(8,128)(2,1)S(1)} %collective-permute-done.4), kind=kOutput, calls=%fused_computation.1 | convolution fusion | flops 537133056 | bytes 6553600 | tf_op jit(solution)/shard_map/dot_general | solution.py:14
  180.9 36.7 %reduce-scatter.14.cloned.1.call-done = f32[256,128]{0,1:T(8,128)} async-done(((f32[2048,128]{0,1:T(8,128)}), f32[256,128]{0,1:T(8,128)}) %reduce-scatter.14.cloned.1.call-update) | async-done | bytes 131088 | tf_op jit(solution)/shard_map/reduce_scatter | solution.py:49
  218.5 7.7 %all_gather.11 = bf16[1024,128]{0,1:T(8,128)(2,1)} all-gather(bf16[256,128]{0,1:T(8,128)(2,1)S(1)} %convert_element_type.47), channel_id=1, replica_groups=mesh['pipe'=4,'dp'=4,'tensor'=8] {'dp'}, dimensions={0}, use_global_device_ids=true | all-gather | bytes 327680 | tf_op jit(solution)/shard_map/all_gather | solution.py:50
  226.2 1.3 collective-permute-start.5
  228.4 9.6 %collective-permute-done.5 = bf16[1024,128]{0,1:T(8,128)(2,1)S(1)} collective-permute-done((bf16[1024,128]{0,1:T(8,128)(2,1)}, bf16[1024,128]{0,1:T(8,128)(2,1)S(1)}, u32[]{:S(2)}, u32[]{:S(2)}) %collective-permute-start.5) | collective-permute-done | bytes 262176 | tf_op jit(solution)/shard_map/ppermute | solution.py:51
  238.0 1.4 convolution_bitcast_fusion
  241.0 2.5 compare_convert_fusion
  243.5 22.3 %reduce-scatter.16.cloned.1.call-done = f32[64,128]{1,0:T(8,128)} async-done(((f32[512,128]{1,0:T(8,128)}), f32[64,128]{1,0:T(8,128)}) %reduce-scatter.16.cloned.1.call-update) | async-done | bytes 32784
  266.6 37.8 %reduce-scatter.18.cloned.1.call-done = f32[64,128]{1,0:T(8,128)} async-done(((f32[512,128]{1,0:T(8,128)}), f32[64,128]{1,0:T(8,128)}) %reduce-scatter.18.cloned.1.call-update) | async-done | bytes 32784
  304.5 0.9 fusion.21
  305.5 1.0 fusion.18
  306.6 8.8 %all_to_all.9 = f32[8,1,1024]{2,1,0:T(1,128)S(1)} all-to-all(f32[8,1,1024]{2,1,0:T(1,128)S(1)} %all_to_all.6), channel_id=1, replica_groups=mesh['pipe'=4,'dp'=4,'tensor'=8] {'tensor'}, dimensions={0} | all-to-all | bytes 65536 | tf_op jit(solution)/shard_map/all_to_all | solution.py:73
  (52 shorter events, 9.8 us)
Async XLA Ops:
  6.5 171.7 %copy-start = (bf16[4,1,128,1024]{3,2,1,0:T(8,128)(2,1)S(1)}, bf16[4,1,128,1024]{3,2,1,0:T(8,128)(2,1)}, u32[]{:S(2)}) copy-start(bf16[4,1,128,1024]{3,2,1,0:T(8,128)(2,1)} %param.9) | copy-start | bytes 3145732
  6.5 85.9 %reduce-scatter.10.cloned.1.call-start = ((), (), s32[]{:S(2)}) async-start(), calls=%async_computation.6 | async-start | bytes 1179648 | tf_op jit(solution)/shard_map/reduce_scatter | solution.py:49
  7.5 28.5 %copy-start.4 = (bf16[128,128]{1,0:T(8,128)(2,1)}, bf16[128,128]{1,0:T(8,128)(2,1)S(1)}, u32[]{:S(2)}) copy-start(bf16[128,128]{1,0:T(8,128)(2,1)S(1)} %add_convert_fusion.1) | copy-start | bytes 98308
  9.3 35.9 %collective-permute-start = (bf16[1024,64]{0,1:T(8,128)(2,1)}, bf16[1024,64]{0,1:T(8,128)(2,1)}, u32[]{:S(2)}, u32[]{:S(2)}) collective-permute-start(bf16[1024,64]{0,1:T(8,128)(2,1)} %convolution_convert_fusion), channel_id=1, source_target_pairs={{0,32},{32,64},{64,96},{1,33},{33,65},{65,97},{2,34},{34,66},{66,9... | collective-permute-start | bytes 393224 | tf_op jit(solution)/shard_map/ppermute | solution.py:45
  35.9 5.8 %copy-start.2 = (bf16[1,128,8192]{2,1,0:T(8,128)(2,1)S(1)}, bf16[1,128,8192]{2,1,0:T(8,128)(2,1)}, u32[]{:S(2)}) copy-start(bf16[1,128,8192]{2,1,0:T(8,128)(2,1)} %param.12) | copy-start | bytes 6291460
  40.7 4.6 %copy-start.1 = (bf16[1,1024,128]{2,1,0:T(8,128)(2,1)S(1)}, bf16[1,1024,128]{2,1,0:T(8,128)(2,1)}, u32[]{:S(2)}) copy-start(bf16[1,1024,128]{2,1,0:T(8,128)(2,1)} %param.11) | copy-start | bytes 786436
  51.3 104.0 %reduce-scatter.12.cloned.1.call-start = ((), (), s32[]{:S(2)}) async-start(), calls=%async_computation.7 | async-start | bytes 1179648 | tf_op jit(solution)/shard_map/reduce_scatter | solution.py:49
  101.1 9.7 %collective-permute-start.2 = (bf16[1024,128]{0,1:T(8,128)(2,1)}, bf16[1024,128]{0,1:T(8,128)(2,1)S(1)}, u32[]{:S(2)}, u32[]{:S(2)}) collective-permute-start(bf16[1024,128]{0,1:T(8,128)(2,1)} %all_gather.9), channel_id=1, source_target_pairs={{0,32},{32,64},{64,96},{1,33},{33,65},{65,97},{2,34},{34,66},{66,9... | collective-permute-start | bytes 786440 | tf_op jit(solution)/shard_map/ppermute | solution.py:53
  116.0 101.5 %reduce-scatter.14.cloned.1.call-start = ((), (), s32[]{:S(2)}) async-start(), calls=%async_computation.8 | async-start | bytes 1179648 | tf_op jit(solution)/shard_map/reduce_scatter | solution.py:49
  163.5 3.5 %copy-start.6 = (bf16[1024,128]{0,1:T(8,128)(2,1)}, bf16[1024,128]{0,1:T(8,128)(2,1)S(1)}, u32[]{:S(2)}) copy-start(bf16[1024,128]{0,1:T(8,128)(2,1)S(1)} %all_gather.10) | copy-start | bytes 786436
  163.5 9.5 %collective-permute-start.4 = (bf16[1024,128]{0,1:T(8,128)(2,1)S(1)}, bf16[1024,128]{0,1:T(8,128)(2,1)S(1)}, u32[]{:S(2)}, u32[]{:S(2)}) collective-permute-start(bf16[1024,128]{0,1:T(8,128)(2,1)S(1)} %all_gather.10), channel_id=1, source_target_pairs={{0,32},{32,64},{64,96},{1,33},{33,65},{65,97},{2,34},{34,66},{66,9... | collective-permute-start | bytes 786440 | tf_op jit(solution)/shard_map/ppermute | solution.py:53
  173.4 5.2 %copy-start.5 = (bf16[128,128]{1,0:T(8,128)(2,1)S(1)}, bf16[128,128]{1,0:T(8,128)(2,1)}, u32[]{:S(2)}) copy-start(bf16[128,128]{1,0:T(8,128)(2,1)} %copy-done.4) | copy-start | bytes 98308
  178.1 59.9 %copy-start.3 = (bf16[4,128,1024]{2,1,0:T(8,128)(2,1)S(1)}, bf16[4,128,1024]{2,1,0:T(8,128)(2,1)}, u32[]{:S(2)}) copy-start(bf16[4,128,1024]{2,1,0:T(8,128)(2,1)} %param.8) | copy-start | bytes 3145732
  178.2 62.1 %copy-start.7 = (s32[4]{0:T(128)S(1)}, s32[4]{0:T(128)}, u32[]{:S(2)}) copy-start(s32[4]{0:T(128)} %param.15) | copy-start | bytes 52
  178.2 87.6 %reduce-scatter.16.cloned.1.call-start = ((), (), s32[]{:S(2)}) async-start(), calls=%async_computation.9 | async-start | bytes 294912
  179.5 48.9 %collective-permute-start.1 = (bf16[1024,128]{0,1:T(8,128)(2,1)}, bf16[1024,128]{0,1:T(8,128)(2,1)S(1)}, u32[]{:S(2)}, u32[]{:S(2)}) collective-permute-start(bf16[1024,128]{0,1:T(8,128)(2,1)} %all_gather.9), channel_id=1, source_target_pairs={{96,64},{97,65},{98,66},{99,67},{100,68},{101,69},{102,70},{103,71... | collective-permute-start | bytes 786440 | tf_op jit(solution)/shard_map/ppermute | solution.py:51
  180.2 48.2 %collective-permute-start.3 = (bf16[1024,128]{0,1:T(8,128)(2,1)}, bf16[1024,128]{0,1:T(8,128)(2,1)S(1)}, u32[]{:S(2)}, u32[]{:S(2)}) collective-permute-start(bf16[1024,128]{0,1:T(8,128)(2,1)} %copy-done.6), channel_id=1, source_target_pairs={{96,32},{97,33},{98,34},{99,35},{100,36},{101,37},{102,38},{103,39... | collective-permute-start | bytes 786440 | tf_op jit(solution)/shard_map/ppermute | solution.py:51
  226.2 11.9 %collective-permute-start.5 = (bf16[1024,128]{0,1:T(8,128)(2,1)}, bf16[1024,128]{0,1:T(8,128)(2,1)S(1)}, u32[]{:S(2)}, u32[]{:S(2)}) collective-permute-start(bf16[1024,128]{0,1:T(8,128)(2,1)} %all_gather.11), channel_id=1, source_target_pairs={{96,0},{97,1},{98,2},{99,3},{100,4},{101,5},{102,6},{103,7},{104,8... | collective-permute-start | bytes 786440 | tf_op jit(solution)/shard_map/ppermute | solution.py:51
  228.4 76.1 %reduce-scatter.18.cloned.1.call-start = ((), (), s32[]{:S(2)}) async-start(), calls=%async_computation.10 | async-start | bytes 294912
Sparse Core Ops, SparseCore 0:
  51.4 40.9 reduce-scatter.9
  116.1 39.1 reduce-scatter.11
  178.3 39.2 reduce-scatter.13
  228.5 37.2 reduce-scatter.15
  268.0 36.4 reduce-scatter.17
where the time goes:
time: 324 us; the launch traced here: 323 us
  waiting for transfers between devices  199 us (61%)
  local copies, waits for them, and re-layouts  34.7 us (11%)
  blocking collectives  31.5 us (10%)
  matrix products  22.6 us (7%)
  starting transfers between devices  13.8 us (4%)
  between operations  13.4 us (4%)
  other arithmetic  7.37 us (2%)
    reduce_scatter x3, waiting for transfers between devices, per_device(): lax.psum_scatter(part, 'tensor', scatter_dimension=0, tiled=True)  117 us
    unnamed x7, waiting for transfers between devices  60.2 us
    unnamed x21, local copies, waits for them, and re-layouts  27.4 us
    all_gather x3, blocking collectives, per_device(): block = lax.all_gather(whole, 'dp', axis=0, tiled=True)  22.7 us
    dot_general x9, matrix products, tn(): lax.dot_general(left, right, (((0,), (0,)), ((), ())), preferred_element_...  20 us
    ppermute x2, waiting for transfers between devices, per_device(): right = lax.ppermute(block, 'pipe', up_one)  12.4 us
    ppermute x3, waiting for transfers between devices, per_device(): lax.ppermute(block, 'pipe', [(sections - 1, sections - 1 - k)])  9.61 us
    all_to_all x1, blocking collectives, per_device(): got = lax.all_to_all(full, 'tensor', 0, 0, tiled=True)  8.8 us
  transfers between devices with their start and end apart: 11, of which 8 were waited for; matrix products, arithmetic and copies ran while one was open for 13% of the time, Pallas kernels for 0%

commit v1 on v0

v1 whole, which is shorter than its diff:
```python
import functools
import math

import jax
import jax.numpy as jnp
from jax import lax
from jax.experimental import pallas as pl
from jax.experimental.pallas import tpu as pltpu
from jax.sharding import PartitionSpec as P

ADAPTER_SCALE = 2.0
F32 = jnp.float32
BF16 = jnp.bfloat16
MESH = pl.DeviceIdType.MESH
SELF = 5


def dot(left, right):
    return jnp.dot(left, right, preferred_element_type=F32)


def nt(left, right):
    return lax.dot_general(left, right, (((1,), (1,)), ((), ())), preferred_element_type=F32)


def tn(left, right, **kw):
    return lax.dot_general(left, right, (((0,), (0,)), ((), ())), preferred_element_type=F32, **kw)


def identity(rows, cols):
    r = lax.broadcasted_iota(jnp.int32, (rows, cols), 0)
    q = lax.broadcasted_iota(jnp.int32, (rows, cols), 1)
    return jnp.where(r == q, 1.0, 0.0).astype(BF16)


def kernel(
    sizes,
    g_hbm, x_hbm, w_hbm, a_hbm, b_hbm, wide_hbm, rank_hbm, len_ref,
    out_ref,
    g_v, x_v, w_v, a_v, b_own, b_out, wide_v, rank_v,
    vbuf, rt, gbuf, part, parts_in, x_out, x_in, y_out, y_in, f_out, f_in,
    load_sem, rt_send, rt_recv, g_send, g_recv, p_send, p_recv,
    x_send, x_recv, y_send, y_recv, f_send, f_recv,
):
    local, proj, seq = sizes
    half = local // 2
    s = lax.axis_index("pipe")
    d = lax.axis_index("dp")
    t = lax.axis_index("tensor")
    zh, c = d // 2, d % 2
    z, x = t // 4, t % 4

    def peer(j, sign):
        dx, dz = (j // 2 + 2) % 4, 1 - j % 2
        return ((z + dz) % 2) * 4 + (x + sign * dx + 4) % 4

    def load(src, dst, i):
        return pltpu.make_async_copy(src, dst, load_sem.at[i])

    def cols_of(u):
        return pl.ds(pl.multiple_of(u * local + c * half, half), half)

    rows = pl.ds(pl.multiple_of(t * local, local), local)
    get_rank = load(rank_hbm, rank_v, 0)
    get_own = load(b_hbm.at[:, cols_of(t)], b_own, 1)
    get_wide = load(wide_hbm.at[rows, :], wide_v, 2)
    get_a = load(a_hbm, a_v, 3)
    get_x = load(x_hbm, x_v, 4)
    get_g = load(g_hbm, g_v, 5)
    get_b = [load(b_hbm.at[:, cols_of(u)], b_out.at[u], 6 + u) for u in range(8)]
    get_w = [load(w_hbm.at[:, cols_of(u)], w_v.at[u], 14 + u) for u in range(8)]
    for copy in (get_rank, get_own, get_wide, get_a, get_x):
        copy.start()

    barrier = pltpu.get_barrier_semaphore()
    for i in range(1, 8):
        pl.semaphore_signal(barrier, inc=1, device_id={"tensor": (t + i) % 8}, device_id_type=MESH)
    for i in range(1, 16):
        there = {"pipe": (s + i // 4) % 4, "dp": (d + i % 4) % 4}
        pl.semaphore_signal(barrier, inc=1, device_id=there, device_id_type=MESH)

    @pl.when(s >= 1)
    def _():
        for copy in get_w + get_b:
            copy.start()

    get_g.start()

    get_rank.wait()
    low = (2 * rank_v[...] - 1).astype(F32).astype(BF16)
    low_t = nt(identity(128, 128), low).astype(BF16)
    get_own.wait()
    bq_t = dot(low_t[:proj], b_own[...])
    get_wide.wait()
    own = wide_v[pl.ds(pl.multiple_of(c * half, half), half), :]
    p_t = nt(identity(proj, proj), (2 * own - 1).astype(F32).astype(BF16))
    vbuf[0] = jnp.where(zh == 0, bq_t, p_t).astype(BF16)

    pl.semaphore_wait(barrier, 22)

    def to_next(k, core):
        return pltpu.make_async_remote_copy(
            src_ref=vbuf.at[k], dst_ref=rt.at[k, c],
            send_sem=rt_send.at[k, core], recv_sem=rt_recv.at[k, c],
            device_id={"pipe": (s + 1) % 4, "dp": zh * 2 + core}, device_id_type=MESH,
        )

    def to_final(k, i):
        there = {"pipe": 3 - k, "dp": (d + i) % 4}
        return pltpu.make_async_remote_copy(
            src_ref=vbuf.at[k], dst_ref=gbuf.at[c, pl.ds(pl.multiple_of(zh * proj, proj), proj)],
            send_sem=g_send.at[k, i], recv_sem=g_recv.at[d],
            device_id=there, device_id_type=MESH,
        )

    def from_final(src):
        place = gbuf.at[src % 2, pl.ds(pl.multiple_of((src // 2) * proj, proj), proj)]
        return pltpu.make_async_remote_copy(
            src_ref=vbuf.at[0], dst_ref=place, send_sem=g_send.at[0, 0], recv_sem=g_recv.at[src],
            device_id={"pipe": s}, device_id_type=MESH,
        )

    def hand_on(k):
        if k < 3:
            @pl.when((s >= k) & (s < 3))
            def _():
                for core in range(2):
                    to_next(k, core).start()

        @pl.when(s == 3)
        def _():
            for i in range(1 if k == 0 else 0, 4):
                to_final(k, i).start()

    hand_on(0)

    @pl.when(s == 3)
    def _():
        gbuf[c, pl.ds(pl.multiple_of(zh * proj, proj), proj)] = vbuf[0]

    def swap(out, into, send, recv, j):
        to = peer(j, 1)
        return pltpu.make_async_remote_copy(
            src_ref=out.at[to], dst_ref=into.at[t], send_sem=send.at[j], recv_sem=recv.at[t],
            device_id={"tensor": to}, device_id_type=MESH,
        )

    def total(out, into, send, recv):
        acc = out[t].astype(F32)
        for j in range(8):
            if j != SELF:
                src = peer(j, -1)
                pltpu.make_async_remote_copy(
                    src_ref=out.at[0], dst_ref=into.at[src], send_sem=send.at[j], recv_sem=recv.at[src],
                    device_id={"tensor": src}, device_id_type=MESH,
                ).wait_recv()
                acc = acc + into[src].astype(F32)
        return acc

    def spread(out, into, send, recv):
        for j in range(8):
            if j != SELF:
                swap(out, into, send, recv, j).start()

    get_a.wait()
    lane = lax.broadcasted_iota(jnp.int32, (128, 128), 1)
    qb_wide = jnp.where(lane >= proj, low.astype(F32), 0.0).astype(BF16)
    signs = (2 * wide_v[...] - 1).astype(F32).astype(BF16)
    proj_x = (dot(signs, identity(proj, 128)) + dot(a_v[...], qb_wide)).astype(BF16)
    get_x.wait()
    xs = dot(x_v[...], proj_x)
    x_out[...] = xs.reshape(x_out.shape).astype(x_out.dtype)
    spread(x_out, x_in, x_send, x_recv)

    for k in range(1, 4):
        @pl.when(s >= k)
        def _(k=k):
            if k == 1:
                for copy in get_w + get_b:
                    copy.wait()
            for core in range(2):
                pltpu.make_async_remote_copy(
                    src_ref=vbuf.at[k - 1], dst_ref=rt.at[k - 1, core],
                    send_sem=rt_send.at[k - 1, core], recv_sem=rt_recv.at[k - 1, core],
                    device_id={"pipe": s}, device_id_type=MESH,
                ).wait_recv()
            r0, r1 = rt[k - 1, 0], rt[k - 1, 1]
            small = dot(r0, a_v[:half]) + dot(r1, a_v[half:])
            small = (ADAPTER_SCALE * small).astype(BF16)

            def piece(j, carry):
                to = peer(j, 1)
                value = dot(r0, w_v[to, :half]) + dot(r1, w_v[to, half:]) + dot(small, b_out[to])
                part[k - 1, to] = value.astype(BF16)

                @pl.when(j != SELF)
                def _():
                    swap(part.at[k - 1], parts_in.at[k - 1], p_send.at[k - 1], p_recv.at[k - 1], j).start()

                return carry

            lax.fori_loop(0, 8, piece, 0)
            vbuf[k] = total(part.at[k - 1], parts_in.at[k - 1], p_send.at[k - 1], p_recv.at[k - 1]).astype(BF16)

        hand_on(k)

    get_g.wait()
    for i in range(4):
        if i == 0:
            @pl.when(s < 3)
            def _():
                from_final(d).wait_recv()
        else:
            from_final((d + i) % 4).wait_recv()
    ys = nt(g_v[:, :half], gbuf[0]) + nt(g_v[:, half:], gbuf[1])
    y_out[...] = ys.reshape(y_out.shape).astype(y_out.dtype)
    spread(y_out, y_in, y_send, y_recv)
    xt = total(x_out, x_in, x_send, x_recv)
    per = xt.shape[0]
    index = lax.broadcasted_iota(jnp.int32, xt.shape, 0) + (t * per) % seq
    scale = ADAPTER_SCALE / math.sqrt(seq) / math.sqrt(local * 8) / math.sqrt(128)
    xt = jnp.where(index < len_ref[(t * per) // seq], xt * scale, 0.0)
    yt = total(y_out, y_in, y_send, y_recv)
    full = tn(xt, yt, precision=lax.Precision.HIGHEST)
    f_out[...] = full.reshape(f_out.shape)
    spread(f_out, f_in, f_send, f_recv)
    f_in[t] = f_out[t]
    for j in range(8):
        if j != SELF:
            src = peer(j, -1)
            pltpu.make_async_remote_copy(
                src_ref=f_out.at[0], dst_ref=f_in.at[src], send_sem=f_send.at[j], recv_sem=f_recv.at[src],
                device_id={"tensor": src}, device_id_type=MESH,
            ).wait_recv()
    for e in range(4):
        out_ref[e] = f_in[2 * e] + f_in[2 * e + 1]

    for k in range(3):
        @pl.when((s >= k) & (s < 3))
        def _(k=k):
            for core in range(2):
                to_next(k, core).wait_send()

    @pl.when(s == 3)
    def _():
        for k in range(4):
            for i in range(1 if k == 0 else 0, 4):
                to_final(k, i).wait_send()

    for k in range(1, 4):
        @pl.when(s >= k)
        def _(k=k):
            for j in range(8):
                if j != SELF:
                    swap(part.at[k - 1], parts_in.at[k - 1], p_send.at[k - 1], p_recv.at[k - 1], j).wait_send()

    for out, into, send, recv in (
        (x_out, x_in, x_send, x_recv), (y_out, y_in, y_send, y_recv), (f_out, f_in, f_send, f_recv),
    ):
        for j in range(8):
            if j != SELF:
                swap(out, into, send, recv, j).wait_send()


def per_device(g, acts, weights, down, up, wide_bits, rank_bits, lengths):
    t = lax.axis_index("tensor")
    count, seq, local = g.shape
    tokens = count * seq
    rank, width = up.shape[1:]
    proj = wide_bits.shape[1]
    half = local // 2
    per = tokens // 8
    dma = pltpu.SemaphoreType.DMA
    hbm = pl.BlockSpec(memory_space=pl.ANY)
    out = pl.pallas_call(
        functools.partial(kernel, (local, proj, seq)),
        out_shape=jax.ShapeDtypeStruct((count, 16, 128), F32),
        in_specs=[hbm] * 7 + [pl.BlockSpec(memory_space=pltpu.SMEM)],
        out_specs=pl.BlockSpec(memory_space=pltpu.VMEM),
        scratch_shapes=[
            pltpu.VMEM((tokens, local), BF16),
            pltpu.VMEM((tokens, local), BF16),
            pltpu.VMEM((8, local, half), BF16),
            pltpu.VMEM((local, rank), BF16),
            pltpu.VMEM((rank, half), BF16),
            pltpu.VMEM((8, rank, half), BF16),
            pltpu.VMEM((local, proj), jnp.int32),
            pltpu.VMEM((rank, 2 * proj), jnp.int32),
            pltpu.VMEM((4, proj, half), BF16),
            pltpu.VMEM((3, 2, proj, half), BF16),
            pltpu.VMEM((2, 2 * proj, half), BF16),
            pltpu.VMEM((3, 8, proj, half), BF16),
            pltpu.VMEM((3, 8, proj, half), BF16),
            pltpu.VMEM((8, per, 128), F32),
            pltpu.VMEM((8, per, 128), F32),
            pltpu.VMEM((8, per, 128), BF16),
            pltpu.VMEM((8, per, 128), BF16),
            pltpu.VMEM((8, 16, 128), F32),
            pltpu.VMEM((8, 16, 128), F32),
            dma((22,)), dma((3, 2)), dma((3, 2)), dma((4, 4)), dma((4,)),
            dma((3, 8)), dma((3, 8)),
            dma((8,)), dma((8,)), dma((8,)), dma((8,)), dma((8,)), dma((8,)),
        ],
        compiler_params=pltpu.CompilerParams(
            collective_id=0, has_side_effects=True, vmem_limit_bytes=48 * 1024 * 1024
        ),
    )(
        g.reshape(tokens, local), acts.reshape(tokens, local), weights[0], down[0], up[0],
        wide_bits, rank_bits, lengths,
    )
    out = jnp.where(t < 4, out[:, :, :proj], out[:, :, proj:])
    return out.reshape(count, 1, 16 * proj)


def solution(mesh):
    placed = (
        P("dp", None, "tensor"),
        P("dp", "pipe", None, "tensor"),
        P("pipe", "tensor", None),
        P("pipe", "tensor", None),
        P("pipe", None, None),
        P(),
        P(),
        P("dp"),
    )
    return jax.shard_map(
        per_device, mesh=mesh, in_specs=placed, out_specs=P("dp", "pipe", "tensor"), check_vma=False
    )
```

time: 324 us -> 74.4 us (0.23)
  waiting for transfers between devices: 199 us -> 0 us
  Pallas kernels: 0 us -> 68.2 us
  blocking collectives: 31.5 us -> 0 us
  local copies, waits for them, and re-layouts: 34.7 us -> 5.86 us
  matrix products: 22.6 us -> 0 us
  starting transfers between devices: 13.8 us -> 0 us
  between operations: 13.4 us -> 0.05 us
  other arithmetic: 7.37 us -> 0.07 us
    reduce_scatter x3 -> x0, waiting for transfers between devices: 117 us -> none  [per_device(): lax.psum_scatter(part, 'tensor', scatter_dimension=0, tiled=True)]
    pallas_call x0 -> x1, Pallas kernels: none -> 68.2 us  [per_device(): pl.pallas_call(functools.partial(kernel, (local, proj, seq)), out_shape=j...]
    unnamed x7 -> x0, waiting for transfers between devices: 60.2 us -> none
    all_gather x3 -> x0, blocking collectives: 22.7 us -> none  [per_device(): block = lax.all_gather(whole, 'dp', axis=0, tiled=True)]
    dot_general x13 -> x0, matrix products: 22.6 us -> none  [the longest x9 20 us: tn(): lax.dot_general(left, right, (((0,), (0,)), ((), ())), preferred_element_...]
    unnamed x21 -> x13, local copies, waits for them, and re-layouts: 27.4 us -> 5.16 us
    ppermute x6 -> x0, waiting for transfers between devices: 22 us -> none  [the longest x2 12.4 us: per_device(): right = lax.ppermute(block, 'pipe', up_one)]
    ppermute x6 -> x0, starting transfers between devices: 13.7 us -> none  [the longest x2 6.81 us: per_device(): right = lax.ppermute(block, 'pipe', up_one)]
  transfers between devices with their start and end apart: 11 -> 0, of which waited for: 8 -> 0; matrix products, arithmetic and copies ran while one was open for 13% -> 0% of each run, Pallas kernels for 0% -> 0%
where the time goes in v1:
time: 74.4 us; the launch traced here: 74.2 us
  Pallas kernels  68.2 us (92%)
  local copies, waits for them, and re-layouts  5.86 us (8%)
    pallas_call x1, Pallas kernels, per_device(): pl.pallas_call(functools.partial(kernel, (local, proj, seq)), out_shape=j...  68.2 us
    unnamed x13, local copies, waits for them, and re-layouts  5.16 us

profile of v1, /device:TPU:0, one launch (start us, length us, event | category | flops | bytes accessed | tf_op | source)
XLA Modules:
  0.0 74.2 jit_solution(2716118042275392396)
XLA Ops:
  0.0 0.0 copy-start.1
  0.0 0.0 copy-start.3
  0.0 0.0 copy-start
  0.0 0.0 copy-start.4
  0.0 0.0 copy-start.5
  0.0 3.9 %copy.9.wide_hbm = s32[8192,64]{1,0:T(8,128)} copy(s32[8192,64]{0,1:T(8,128)} %param.13) | data formatting | bytes 4194304 | tf_op args[5]
  3.9 0.0 copy-done.1
  3.9 0.0 copy-done.3
  3.9 0.0 copy-done
  3.9 0.0 copy-done.4
  4.0 0.0 copy-done.5
  4.0 0.0 copy-start.2
  4.0 1.2 %copy-done.2 = bf16[4,1,128,1024]{3,2,1,0:T(8,128)(2,1)S(1)} copy-done((bf16[4,1,128,1024]{3,2,1,0:T(8,128)(2,1)S(1)}, bf16[4,1,128,1024]{3,2,1,0:T(8,128)(2,1)}, u32[]{:S(2)}) %copy-start.2) | copy-done | bytes 1048600
  5.2 68.2 %shard_map.82 = f32[4,16,128]{2,1,0:T(8,128)S(1)} custom-call(bf16[512,1024]{1,0:T(8,128)(2,1)S(1)} %bitcast.6, bf16[512,1024]{1,0:T(8,128)(2,1)S(1)} %bitcast.7, bf16[1024,8192]{1,0:T(8,128)(2,1)} %bitcast.9, bf16[1024,128]{1,0:T(8,128)(2,1)S(1)} %bitcast.8, bf16[128,8192]{1,0:T(8,128)(2,1)S(1)} %bitcast.5, s32[8192,64]{1,0:T(8,128)} %copy.9.wide_hbm, ...), custom_call_target="tpu_custom_call" | custom-call | tf_op jit(solution)/shard_map/pallas_call | solution.py:275
  73.4 0.1 slice_select_fusion
  73.5 0.7 reshape.12
Async XLA Ops:
  0.0 3.9 %copy-start.1 = (bf16[4,128,1024]{2,1,0:T(8,128)(2,1)S(1)}, bf16[4,128,1024]{2,1,0:T(8,128)(2,1)}, u32[]{:S(2)}) copy-start(bf16[4,128,1024]{2,1,0:T(8,128)(2,1)} %param.8) | copy-start | bytes 3145732
  0.0 3.9 %copy-start.3 = (bf16[1,1024,128]{2,1,0:T(8,128)(2,1)S(1)}, bf16[1,1024,128]{2,1,0:T(8,128)(2,1)}, u32[]{:S(2)}) copy-start(bf16[1,1024,128]{2,1,0:T(8,128)(2,1)} %param.11) | copy-start | bytes 786436
  0.0 3.9 %copy-start = (bf16[1,128,8192]{2,1,0:T(8,128)(2,1)S(1)}, bf16[1,128,8192]{2,1,0:T(8,128)(2,1)}, u32[]{:S(2)}) copy-start(bf16[1,128,8192]{2,1,0:T(8,128)(2,1)} %param.12) | copy-start | bytes 6291460
  0.0 3.9 %copy-start.4 = (s32[128,128]{1,0:T(8,128)S(1)}, s32[128,128]{1,0:T(8,128)}, u32[]{:S(2)}) copy-start(s32[128,128]{1,0:T(8,128)} %rank_hbm.1) | copy-start | bytes 196612
  0.0 4.0 %copy-start.5 = (s32[4]{0:T(128)S(1)}, s32[4]{0:T(128)}, u32[]{:S(2)}) copy-start(s32[4]{0:T(128)} %len_ref.1) | copy-start | bytes 52
  4.0 1.2 %copy-start.2 = (bf16[4,1,128,1024]{3,2,1,0:T(8,128)(2,1)S(1)}, bf16[4,1,128,1024]{3,2,1,0:T(8,128)(2,1)}, u32[]{:S(2)}) copy-start(bf16[4,1,128,1024]{3,2,1,0:T(8,128)(2,1)} %param.9) | copy-start | bytes 3145732

commit v2 on v1

v2 whole, which is shorter than its diff:
```python
import functools
import math

import jax
import jax.numpy as jnp
from jax import lax
from jax.experimental import pallas as pl
from jax.experimental.pallas import tpu as pltpu
from jax.sharding import PartitionSpec as P

ADAPTER_SCALE = 2.0
F32 = jnp.float32
BF16 = jnp.bfloat16
MESH = pl.DeviceIdType.MESH
SELF = 5
YP, UQ = 0, 1


def dot(left, right):
    return jnp.dot(left, right, preferred_element_type=F32)


def nt(left, right, **kw):
    return lax.dot_general(left, right, (((1,), (1,)), ((), ())), preferred_element_type=F32, **kw)


def identity(n):
    r = lax.broadcasted_iota(jnp.int32, (n, n), 0)
    q = lax.broadcasted_iota(jnp.int32, (n, n), 1)
    return jnp.where(r == q, 1.0, 0.0).astype(BF16)


def signs_of(bits):
    return (2 * bits - 1).astype(F32).astype(BF16)


def kernel(
    sizes,
    g_hbm, x_hbm, w_hbm, a_hbm, b_hbm, wide_hbm, rank_hbm, len_ref,
    out_ref,
    g_v, x_v, w_v, a_v, b_own, b_out, wide_v, rank_v, low_v,
    vbuf, rt, gbuf, part, parts_in, x_out, x_in, y_out, y_in, y_sum, f_out, f_in,
    load_sem, rt_send, rt_recv, g_send, g_recv, p_send, p_recv,
    x_send, x_recv, y_send, y_recv, f_send, f_recv,
):
    local, proj, seq = sizes
    half, cols = local // 2, proj // 2
    s = lax.axis_index("pipe")
    d = lax.axis_index("dp")
    t = lax.axis_index("tensor")
    zh, c = d // 2, d % 2
    z, x = t // 4, t % 4

    def peer(j, sign):
        dx, dz = (j // 2 + 2) % 4, 1 - j % 2
        return ((z + dz) % 2) * 4 + (x + sign * dx + 4) % 4

    def load(src, dst, i):
        return pltpu.make_async_copy(src, dst, load_sem.at[i])

    def cols_of(u):
        return pl.ds(pl.multiple_of(u * local + c * half, half), half)

    block = pl.ds(pl.multiple_of(t * local, local), local)
    my_cols = pl.ds(pl.multiple_of(zh * cols, cols), cols)
    get_rank = load(rank_hbm, rank_v, 0)
    get_own = load(b_hbm.at[:, block], b_own, 1)
    get_wide = load(wide_hbm.at[:, block], wide_v, 2)
    get_a = load(a_hbm, a_v, 3)
    get_x = load(x_hbm, x_v, 4)
    get_g = load(g_hbm, g_v, 5)
    get_b = [load(b_hbm.at[:, cols_of(u)], b_out.at[u], 6 + u) for u in range(8)]
    get_w = [load(w_hbm.at[:, cols_of(u)], w_v.at[u], 14 + u) for u in range(8)]
    for copy in (get_rank, get_own, get_wide, get_a, get_x):
        copy.start()

    barrier = pltpu.get_barrier_semaphore()
    for i in range(1, 16):
        there = {"pipe": (s + i // 4) % 4, "dp": (d + i % 4) % 4}
        pl.semaphore_signal(barrier, inc=1, device_id=there, device_id_type=MESH)
    for i in range(1, 8):
        pl.semaphore_signal(barrier, inc=1, device_id={"tensor": (t + i) % 8}, device_id_type=MESH)

    @pl.when(s >= 1)
    def _():
        for copy in get_w + get_b:
            copy.start()

    get_g.start()

    get_rank.wait()
    low_v[...] = nt(identity(128), signs_of(rank_v[...])).astype(BF16)
    get_own.wait()
    mine = b_own[:, pl.ds(pl.multiple_of(c * half, half), half)]
    vbuf[UQ, 0] = dot(low_v[my_cols], mine).astype(BF16)
    get_wide.wait()
    p_t = signs_of(wide_v[...])

    @pl.when(s >= 1)
    def _():
        few = signs_of(wide_v[my_cols, :])
        rt[YP, 0, 0] = few[:, :half]
        rt[YP, 0, 1] = few[:, half:]

    @pl.when(s == 3)
    def _():
        bq_t = dot(low_v[:proj], b_own[...]).astype(BF16)
        for h in range(2):
            gbuf[YP, h] = p_t[:, h * half : (h + 1) * half]
            gbuf[UQ, h] = bq_t[:, h * half : (h + 1) * half]

    get_a.wait()
    ab_t = nt(low_v[proj:], a_v[...]).astype(BF16)
    get_x.wait()
    for zz, left in ((0, p_t), (1, ab_t)):
        xs = nt(left, x_v[...]).astype(BF16)
        for e in range(4):
            x_out[zz * 4 + e] = xs[:, e * seq : (e + 1) * seq]

    pl.semaphore_wait(barrier, 22)

    def to_next(ch, k, core):
        return pltpu.make_async_remote_copy(
            src_ref=vbuf.at[ch, k], dst_ref=rt.at[ch, k, c],
            send_sem=rt_send.at[ch, k, core], recv_sem=rt_recv.at[ch, k, c],
            device_id={"pipe": (s + 1) % 4, "dp": zh * 2 + core}, device_id_type=MESH,
        )

    def to_final(ch, k, i):
        return pltpu.make_async_remote_copy(
            src_ref=vbuf.at[ch, k], dst_ref=gbuf.at[ch, c, my_cols],
            send_sem=g_send.at[ch, k, i], recv_sem=g_recv.at[ch, d],
            device_id={"pipe": 3 - k, "dp": (d + i) % 4}, device_id_type=MESH,
        )

    def hand_on(ch, k):
        if k < 3:
            @pl.when((s >= k) & (s < 3))
            def _():
                for core in range(2):
                    to_next(ch, k, core).start()
        if k > 0:
            @pl.when(s == 3)
            def _():
                for i in range(4):
                    to_final(ch, k, i).start()

    def swap(out, into, send, recv, j):
        to = peer(j, 1)
        return pltpu.make_async_remote_copy(
            src_ref=out.at[to], dst_ref=into.at[t], send_sem=send.at[j], recv_sem=recv.at[t],
            device_id={"tensor": to}, device_id_type=MESH,
        )

    def total(out, into, send, recv):
        acc = out[t].astype(F32)
        for j in range(8):
            if j != SELF:
                src = peer(j, -1)
                pltpu.make_async_remote_copy(
                    src_ref=out.at[0], dst_ref=into.at[src], send_sem=send.at[j], recv_sem=recv.at[src],
                    device_id={"tensor": src}, device_id_type=MESH,
                ).wait_recv()
                acc = acc + into[src].astype(F32)
        return acc

    hand_on(UQ, 0)
    for j in range(8):
        if j != SELF:
            swap(x_out, x_in, x_send, x_recv, j).start()

    def group(ch, k):
        i = k - 1
        return part.at[ch, i], parts_in.at[ch, i], p_send.at[ch, i], p_recv.at[ch, i]

    def multiply(ch, k):
        i = k - 1
        if ch == UQ or k > 1:
            for core in range(2):
                pltpu.make_async_remote_copy(
                    src_ref=vbuf.at[ch, i], dst_ref=rt.at[ch, i, core],
                    send_sem=rt_send.at[ch, i, core], recv_sem=rt_recv.at[ch, i, core],
                    device_id={"pipe": (s + 1) % 4}, device_id_type=MESH,
                ).wait_recv()
        r0, r1 = rt[ch, i, 0], rt[ch, i, 1]
        small = dot(r0, a_v[:half]) + dot(r1, a_v[half:])
        small = (ADAPTER_SCALE * small).astype(BF16)

        def piece(j, carry):
            to = peer(j, 1)
            value = dot(r0, w_v[to, :half]) + dot(r1, w_v[to, half:]) + dot(small, b_out[to])
            part[ch, i, to] = value.astype(BF16)

            @pl.when(j != SELF)
            def _():
                swap(*group(ch, k), j).start()

            return carry

        lax.fori_loop(0, 8, piece, 0)

    for k in range(1, 4):
        @pl.when(s >= k)
        def _(k=k):
            if k == 1:
                for copy in get_w + get_b:
                    copy.wait()
            for ch in (YP, UQ):
                multiply(ch, k)
            for ch in (YP, UQ):
                vbuf[ch, k] = total(*group(ch, k)).astype(BF16)
                hand_on(ch, k)

    def y_swap(ch, i):
        e = (x + i) % 4
        to = (1 - ch) * 4 + e
        return pltpu.make_async_remote_copy(
            src_ref=y_out.at[to], dst_ref=y_in.at[t], send_sem=y_send.at[ch, i], recv_sem=y_recv.at[t],
            device_id={"tensor": to}, device_id_type=MESH,
        )

    def y_each(ch, act):
        for i in (2, 1, 3):
            act(y_swap(ch, i))

        @pl.when(z == ch)
        def _():
            act(y_swap(ch, 0))

    xt = total(x_out, x_in, x_send, x_recv)
    token = lax.broadcasted_iota(jnp.int32, xt.shape, 1)
    scale = ADAPTER_SCALE / math.sqrt(seq) / math.sqrt(local * 8) / math.sqrt(128)
    xt = jnp.where(token < len_ref[x], xt * scale, 0.0)
    y_sum[...] = jnp.zeros_like(y_sum)

    get_g.wait()
    for ch in (YP, UQ):
        @pl.when(s < 3)
        def _(ch=ch):
            for src in range(4):
                place = gbuf.at[ch, src % 2, pl.ds((src // 2) * cols, cols)]
                pltpu.make_async_remote_copy(
                    src_ref=vbuf.at[ch, 0], dst_ref=place,
                    send_sem=g_send.at[ch, 0, 0], recv_sem=g_recv.at[ch, src],
                    device_id={"pipe": (s + 1) % 4}, device_id_type=MESH,
                ).wait_recv()

        ys = nt(gbuf[ch, 0], g_v[:, :half]) + nt(gbuf[ch, 1], g_v[:, half:])
        ys = ys.astype(BF16)
        for e in range(4):
            y_out[(1 - ch) * 4 + e] = ys[:, e * seq : (e + 1) * seq]
        y_each(ch, lambda copy: copy.start())

    y_sum[:proj] = total(y_out, y_in, y_send.at[0], y_recv)
    f_out[...] = nt(xt, y_sum[...], precision=lax.Precision.HIGHEST).reshape(f_out.shape)

    def f_swap(i):
        to = (x + i) % 4
        return pltpu.make_async_remote_copy(
            src_ref=f_out.at[to], dst_ref=f_in.at[x], send_sem=f_send.at[i], recv_sem=f_recv.at[x],
            device_id={"tensor": z * 4 + to}, device_id_type=MESH,
        )

    for i in (2, 1, 3):
        f_swap(i).start()
    f_in[x] = f_out[x]
    for i in (2, 1, 3):
        src = (x + i) % 4
        pltpu.make_async_remote_copy(
            src_ref=f_out.at[0], dst_ref=f_in.at[src], send_sem=f_send.at[i], recv_sem=f_recv.at[src],
            device_id={"tensor": z * 4 + src}, device_id_type=MESH,
        ).wait_recv()
    out_ref[...] = f_in[...]

    for ch in (YP, UQ):
        for k in range(1 if ch == YP else 0, 3):
            @pl.when((s >= k) & (s < 3))
            def _(ch=ch, k=k):
                for core in range(2):
                    to_next(ch, k, core).wait_send()

        @pl.when(s == 3)
        def _(ch=ch):
            for k in range(1, 4):
                for i in range(4):
                    to_final(ch, k, i).wait_send()

        for k in range(1, 4):
            @pl.when(s >= k)
            def _(ch=ch, k=k):
                for j in range(8):
                    if j != SELF:
                        swap(*group(ch, k), j).wait_send()

        y_each(ch, lambda copy: copy.wait_send())

    for j in range(8):
        if j != SELF:
            swap(x_out, x_in, x_send, x_recv, j).wait_send()
    for i in (2, 1, 3):
        f_swap(i).wait_send()


def per_device(g, acts, weights, down, up, wide_bits, rank_bits, lengths):
    count, seq, local = g.shape
    tokens = count * seq
    rank = up.shape[1]
    proj = wide_bits.shape[1]
    half, cols = local // 2, proj // 2
    dma = pltpu.SemaphoreType.DMA
    hbm = pl.BlockSpec(memory_space=pltpu.HBM)
    out = pl.pallas_call(
        functools.partial(kernel, (local, proj, seq)),
        out_shape=jax.ShapeDtypeStruct((count, 16, 128), F32),
        in_specs=[hbm] * 7 + [pl.BlockSpec(memory_space=pltpu.SMEM)],
        out_specs=pl.BlockSpec(memory_space=pltpu.VMEM),
        scratch_shapes=[
            pltpu.VMEM((tokens, local), BF16),
            pltpu.VMEM((tokens, local), BF16),
            pltpu.VMEM((8, local, half), BF16),
            pltpu.VMEM((local, rank), BF16),
            pltpu.VMEM((rank, local), BF16),
            pltpu.VMEM((8, rank, half), BF16),
            pltpu.VMEM((proj, local), jnp.int32),
            pltpu.VMEM((rank, 2 * proj), jnp.int32),
            pltpu.VMEM((rank, 2 * proj), BF16),
            pltpu.VMEM((2, 4, cols, half), BF16),
            pltpu.VMEM((2, 3, 2, cols, half), BF16),
            pltpu.VMEM((2, 2, proj, half), BF16),
            pltpu.VMEM((2, 3, 8, cols, half), BF16),
            pltpu.VMEM((2, 3, 8, cols, half), BF16),
            pltpu.VMEM((8, proj, seq), BF16),
            pltpu.VMEM((8, proj, seq), BF16),
            pltpu.VMEM((8, proj, seq), BF16),
            pltpu.VMEM((8, proj, seq), BF16),
            pltpu.VMEM((2 * proj, seq), F32),
            pltpu.VMEM((4, 16, 128), F32),
            pltpu.VMEM((4, 16, 128), F32),
            dma((22,)), dma((2, 3, 2)), dma((2, 3, 2)), dma((2, 4, 4)), dma((2, 4)),
            dma((2, 3, 8)), dma((2, 3, 8)),
            dma((8,)), dma((8,)), dma((2, 8)), dma((8,)), dma((4,)), dma((4,)),
        ],
        compiler_params=pltpu.CompilerParams(
            collective_id=0, has_side_effects=True, vmem_limit_bytes=63 * 1024 * 1024
        ),
    )(
        g.reshape(tokens, local), acts.reshape(tokens, local), weights[0], down[0], up[0],
        wide_bits.T, rank_bits, lengths,
    )
    return out[:, :, :proj].reshape(count, 1, 16 * proj)


def solution(mesh):
    placed = (
        P("dp", None, "tensor"),
        P("dp", "pipe", None, "tensor"),
        P("pipe", "tensor", None),
        P("pipe", "tensor", None),
        P("pipe", None, None),
        P(),
        P(),
        P("dp"),
    )
    return jax.shard_map(
        per_device, mesh=mesh, in_specs=placed, out_specs=P("dp", "pipe", "tensor"), check_vma=False
    )
```

time: 74.4 us -> 60 us (0.81)
  Pallas kernels: 68.2 us -> 58.3 us
  local copies, waits for them, and re-layouts: 5.86 us -> 1.45 us
    pallas_call x1, Pallas kernels: 68.2 us -> 58.3 us  [per_device(): pl.pallas_call(functools.partial(kernel, (local, proj, seq)), out_shape=j...]
    unnamed x13 -> x0, local copies, waits for them, and re-layouts: 5.16 us -> none
    reshape x1, local copies, waits for them, and re-layouts: 0.7 us -> 1.45 us  [per_device(): return out[:, :, :proj].reshape(count, 1, 16 * proj)]
where the time goes in v2:
time: 60 us; the launch traced here: 59.8 us
  Pallas kernels  58.3 us (97%)
  local copies, waits for them, and re-layouts  1.45 us (2%)
    pallas_call x1, Pallas kernels, per_device(): pl.pallas_call(functools.partial(kernel, (local, proj, seq)), out_shape=j...  58.3 us
    reshape x1, local copies, waits for them, and re-layouts, per_device(): return out[:, :, :proj].reshape(count, 1, 16 * proj)  1.45 us

profile of v2, /device:TPU:0, one launch (start us, length us, event | category | flops | bytes accessed | tf_op | source)
XLA Modules:
  0.0 59.8 jit_solution(4919760348851310998)
XLA Ops:
  0.0 58.3 %shard_map.82 = f32[4,16,128]{2,1,0:T(8,128)} custom-call(bf16[512,1024]{1,0:T(8,128)(2,1)} %bitcast.10, bf16[512,1024]{1,0:T(8,128)(2,1)} %bitcast.11, bf16[1024,8192]{1,0:T(8,128)(2,1)} %bitcast.7, bf16[1024,128]{1,0:T(8,128)(2,1)} %bitcast.12, bf16[128,8192]{1,0:T(8,128)(2,1)} %bitcast.8, s32[64,8192]{1,0:T(8,128)} %bitcast.9, s32[128,128]{1,0:T(8,128)} %rank_hbm.1, ...), custom_call_target="tpu_custom_call" | custom-call | tf_op jit(solution)/shard_map/pallas_call | solution.py:312
  58.3 1.4 %reshape.12 = f32[4,1,1024]{2,1,0:T(1,128)} reshape(f32[4,16,64]{2,1,0:T(8,128)} %bitcast.13) | data formatting | bytes 32768 | tf_op jit(solution)/shard_map/reshape | solution.py:350

commit v3 on v2

--- a/solution.py
+++ b/solution.py
@@ -24,10 +24,13 @@
     return lax.dot_general(left, right, (((1,), (1,)), ((), ())), preferred_element_type=F32, **kw)
 
 
-def identity(n):
+def reorder(n, first):
     r = lax.broadcasted_iota(jnp.int32, (n, n), 0)
     q = lax.broadcasted_iota(jnp.int32, (n, n), 1)
-    return jnp.where(r == q, 1.0, 0.0).astype(BF16)
+    half = (n - first) // 2
+    even = first + 2 * (r - first)
+    from_row = jnp.where(r < first, r, jnp.where(r < first + half, even, even - 2 * half + 1))
+    return jnp.where(q == from_row, 1.0, 0.0).astype(BF16)
 
 
 def signs_of(bits):
@@ -39,9 +42,9 @@
     g_hbm, x_hbm, w_hbm, a_hbm, b_hbm, wide_hbm, rank_hbm, len_ref,
     out_ref,
     g_v, x_v, w_v, a_v, b_own, b_out, wide_v, rank_v, low_v,
-    vbuf, rt, gbuf, part, parts_in, x_out, x_in, y_out, y_in, y_sum, f_out, f_in,
+    vbuf, rt, gbuf, part, parts_in, x_out, x_in, x_sum, x_use, y_out, y_in, y_sum, f_out, f_in,
     load_sem, rt_send, rt_recv, g_send, g_recv, p_send, p_recv,
-    x_send, x_recv, y_send, y_recv, f_send, f_recv,
+    x_send, x_recv, xs_send, xs_recv, y_send, y_recv, f_send, f_recv,
 ):
     local, proj, seq = sizes
     half, cols = local // 2, proj // 2
@@ -50,6 +53,8 @@
     t = lax.axis_index("tensor")
     zh, c = d // 2, d % 2
     z, x = t // 4, t % 4
+    edge = 1 - ((s + 1) % 4) // 2
+    home = s + edge * (3 - 2 * s)
 
     def peer(j, sign):
         dx, dz = (j // 2 + 2) % 4, 1 - j % 2
@@ -80,6 +85,9 @@
         pl.semaphore_signal(barrier, inc=1, device_id=there, device_id_type=MESH)
     for i in range(1, 8):
         pl.semaphore_signal(barrier, inc=1, device_id={"tensor": (t + i) % 8}, device_id_type=MESH)
+    for i in range(1, 4):
+        there = {"pipe": 3 - s, "tensor": z * 4 + (x + i) % 4}
+        pl.semaphore_signal(barrier, inc=1, device_id=there, device_id_type=MESH)
 
     @pl.when(s >= 1)
     def _():
@@ -89,12 +97,11 @@
     get_g.start()
 
     get_rank.wait()
-    low_v[...] = nt(identity(128), signs_of(rank_v[...])).astype(BF16)
+    low_v[...] = nt(reorder(128, proj), signs_of(rank_v[...])).astype(BF16)
     get_own.wait()
     mine = b_own[:, pl.ds(pl.multiple_of(c * half, half), half)]
     vbuf[UQ, 0] = dot(low_v[my_cols], mine).astype(BF16)
     get_wide.wait()
-    p_t = signs_of(wide_v[...])
 
     @pl.when(s >= 1)
     def _():
@@ -102,22 +109,14 @@
         rt[YP, 0, 0] = few[:, :half]
         rt[YP, 0, 1] = few[:, half:]
 
-    @pl.when(s == 3)
-    def _():
-        bq_t = dot(low_v[:proj], b_own[...]).astype(BF16)
-        for h in range(2):
-            gbuf[YP, h] = p_t[:, h * half : (h + 1) * half]
-            gbuf[UQ, h] = bq_t[:, h * half : (h + 1) * half]
+    @pl.when(s == 0)
+    def _():
+        p_t = signs_of(wide_v[...])
+        gbuf[YP, 0] = p_t[:, :half]
+        gbuf[YP, 1] = p_t[:, half:]
 
     get_a.wait()
-    ab_t = nt(low_v[proj:], a_v[...]).astype(BF16)
-    get_x.wait()
-    for zz, left in ((0, p_t), (1, ab_t)):
-        xs = nt(left, x_v[...]).astype(BF16)
-        for e in range(4):
-            x_out[zz * 4 + e] = xs[:, e * seq : (e + 1) * seq]
-
-    pl.semaphore_wait(barrier, 22)
+    pl.semaphore_wait(barrier, 25)
 
     def to_next(ch, k, core):
         return pltpu.make_async_remote_copy(
@@ -130,8 +129,11 @@
         return pltpu.make_async_remote_copy(
             src_ref=vbuf.at[ch, k], dst_ref=gbuf.at[ch, c, my_cols],
             send_sem=g_send.at[ch, k, i], recv_sem=g_recv.at[ch, d],
-            device_id={"pipe": 3 - k, "dp": (d + i) % 4}, device_id_type=MESH,
+            device_id={"pipe": (0, 2, 1, 3)[k], "dp": (d + i) % 4}, device_id_type=MESH,
         )
+
+    def final_order(k):
+        return (2, 1, 3) if k == 3 else (2, 1, 3, 0)
 
     def hand_on(ch, k):
         if k < 3:
@@ -139,10 +141,12 @@
             def _():
                 for core in range(2):
                     to_next(ch, k, core).start()
-        if k > 0:
+        if ch == UQ or k > 0:
             @pl.when(s == 3)
             def _():
-                for i in range(4):
+                if k == 3:
+                    gbuf[ch, c, my_cols] = vbuf[ch, k]
+                for i in final_order(k):
                     to_final(ch, k, i).start()
 
     def swap(out, into, send, recv, j):
@@ -165,9 +169,39 @@
         return acc
 
     hand_on(UQ, 0)
-    for j in range(8):
-        if j != SELF:
-            swap(x_out, x_in, x_send, x_recv, j).start()
+
+    def project_x():
+        get_x.wait()
+        p_t = dot(reorder(proj, 0), signs_of(wide_v[...])).astype(BF16)
+        ab_t = nt(low_v[proj:], a_v[...]).astype(BF16)
+        for zz, left in ((0, p_t), (1, ab_t)):
+            xs = nt(left, x_v[...]).astype(BF16)
+            for e in range(4):
+                x_out[zz * 4 + e] = xs[:, e * seq : (e + 1) * seq]
+        for j in range(8):
+            if j != SELF:
+                swap(x_out, x_in, x_send, x_recv, j).start()
+
+    x_cross = pltpu.make_async_remote_copy(
+        src_ref=x_sum, dst_ref=x_use, send_sem=xs_send, recv_sem=xs_recv,
+        device_id={"pipe": home}, device_id_type=MESH,
+    )
+
+    def sum_x():
+        x_sum[...] = total(x_out, x_in, x_send, x_recv)
+
+        @pl.when(edge == 1)
+        def _():
+            x_cross.start()
+
+        @pl.when(edge == 0)
+        def _():
+            x_use[...] = x_sum[...]
+
+    @pl.when(s == 0)
+    def _():
+        project_x()
+        sum_x()
 
     def group(ch, k):
         i = k - 1
@@ -186,18 +220,12 @@
         small = dot(r0, a_v[:half]) + dot(r1, a_v[half:])
         small = (ADAPTER_SCALE * small).astype(BF16)
 
-        def piece(j, carry):
+        for j in range(8):
             to = peer(j, 1)
             value = dot(r0, w_v[to, :half]) + dot(r1, w_v[to, half:]) + dot(small, b_out[to])
             part[ch, i, to] = value.astype(BF16)
-
-            @pl.when(j != SELF)
-            def _():
+            if j != SELF:
                 swap(*group(ch, k), j).start()
-
-            return carry
-
-        lax.fori_loop(0, 8, piece, 0)
 
     for k in range(1, 4):
         @pl.when(s >= k)
@@ -210,6 +238,10 @@
             for ch in (YP, UQ):
                 vbuf[ch, k] = total(*group(ch, k)).astype(BF16)
                 hand_on(ch, k)
+                if ch == YP and k == 1:
+                    project_x()
+                if ch == YP and k == 2:
+                    sum_x()
 
     def y_swap(ch, i):
         e = (x + i) % 4
@@ -227,7 +259,15 @@
         def _():
             act(y_swap(ch, 0))
 
-    xt = total(x_out, x_in, x_send, x_recv)
+    @pl.when(s == 1)
+    def _():
+        sum_x()
+
+    @pl.when(edge == 1)
+    def _():
+        x_cross.wait_recv()
+
+    xt = x_use[...]
     token = lax.broadcasted_iota(jnp.int32, xt.shape, 1)
     scale = ADAPTER_SCALE / math.sqrt(seq) / math.sqrt(local * 8) / math.sqrt(128)
     xt = jnp.where(token < len_ref[x], xt * scale, 0.0)
@@ -235,15 +275,22 @@
 
     get_g.wait()
     for ch in (YP, UQ):
-        @pl.when(s < 3)
-        def _(ch=ch):
-            for src in range(4):
-                place = gbuf.at[ch, src % 2, pl.ds((src // 2) * cols, cols)]
-                pltpu.make_async_remote_copy(
-                    src_ref=vbuf.at[ch, 0], dst_ref=place,
-                    send_sem=g_send.at[ch, 0, 0], recv_sem=g_recv.at[ch, src],
-                    device_id={"pipe": (s + 1) % 4}, device_id_type=MESH,
-                ).wait_recv()
+        def arrived(src, ch=ch):
+            place = gbuf.at[ch, src % 2, pl.ds(pl.multiple_of((src // 2) * cols, cols), cols)]
+            pltpu.make_async_remote_copy(
+                src_ref=vbuf.at[ch, 0], dst_ref=place,
+                send_sem=g_send.at[ch, 0, 0], recv_sem=g_recv.at[ch, src],
+                device_id={"pipe": (s + 1) % 4}, device_id_type=MESH,
+            ).wait_recv()
+
+        @pl.when((s < 3) & (s >= (1 if ch == YP else 0)))
+        def _():
+            arrived(d)
+
+        @pl.when(s >= (1 if ch == YP else 0))
+        def _():
+            for i in range(1, 4):
+                arrived((d + i) % 4)
 
         ys = nt(gbuf[ch, 0], g_v[:, :half]) + nt(gbuf[ch, 1], g_v[:, half:])
         ys = ys.astype(BF16)
@@ -251,25 +298,41 @@
             y_out[(1 - ch) * 4 + e] = ys[:, e * seq : (e + 1) * seq]
         y_each(ch, lambda copy: copy.start())
 
-    y_sum[:proj] = total(y_out, y_in, y_send.at[0], y_recv)
-    f_out[...] = nt(xt, y_sum[...], precision=lax.Precision.HIGHEST).reshape(f_out.shape)
+    yt = total(y_out, y_in, y_send.at[0], y_recv)
+    y_sum[0, :proj] = yt
+    y_sum[1, proj:] = yt
+    exact = lax.Precision.HIGHEST
+    full = nt(xt[:cols], y_sum[0], precision=exact) + nt(xt[cols:], y_sum[1], precision=exact)
+    f_out[...] = full.reshape(f_out.shape)
 
     def f_swap(i):
         to = (x + i) % 4
         return pltpu.make_async_remote_copy(
             src_ref=f_out.at[to], dst_ref=f_in.at[x], send_sem=f_send.at[i], recv_sem=f_recv.at[x],
-            device_id={"tensor": z * 4 + to}, device_id_type=MESH,
+            device_id={"pipe": home, "tensor": z * 4 + to}, device_id_type=MESH,
         )
 
-    for i in (2, 1, 3):
-        f_swap(i).start()
-    f_in[x] = f_out[x]
-    for i in (2, 1, 3):
+    def f_arrived(i):
         src = (x + i) % 4
         pltpu.make_async_remote_copy(
             src_ref=f_out.at[0], dst_ref=f_in.at[src], send_sem=f_send.at[i], recv_sem=f_recv.at[src],
-            device_id={"tensor": z * 4 + src}, device_id_type=MESH,
+            device_id={"pipe": home, "tensor": z * 4 + (x + 1) % 4}, device_id_type=MESH,
         ).wait_recv()
+
+    for i in (2, 1, 3):
+        f_swap(i).start()
+
+    @pl.when(edge == 1)
+    def _():
+        f_swap(0).start()
+        f_arrived(0)
+
+    @pl.when(edge == 0)
+    def _():
+        f_in[x] = f_out[x]
+
+    for i in (1, 3, 2):
+        f_arrived(i)
     out_ref[...] = f_in[...]
 
     for ch in (YP, UQ):
@@ -281,8 +344,8 @@
 
         @pl.when(s == 3)
         def _(ch=ch):
-            for k in range(1, 4):
-                for i in range(4):
+            for k in range(1 if ch == YP else 0, 4):
+                for i in final_order(k):
                     to_final(ch, k, i).wait_send()
 
         for k in range(1, 4):
@@ -299,6 +362,11 @@
             swap(x_out, x_in, x_send, x_recv, j).wait_send()
     for i in (2, 1, 3):
         f_swap(i).wait_send()
+
+    @pl.when(edge == 1)
+    def _():
+        f_swap(0).wait_send()
+        x_cross.wait_send()
 
 
 def per_device(g, acts, weights, down, up, wide_bits, rank_bits, lengths):
@@ -311,7 +379,7 @@
     hbm = pl.BlockSpec(memory_space=pltpu.HBM)
     out = pl.pallas_call(
         functools.partial(kernel, (local, proj, seq)),
-        out_shape=jax.ShapeDtypeStruct((count, 16, 128), F32),
+        out_shape=jax.ShapeDtypeStruct((count, 8, 128), F32),
         in_specs=[hbm] * 7 + [pl.BlockSpec(memory_space=pltpu.SMEM)],
         out_specs=pl.BlockSpec(memory_space=pltpu.VMEM),
         scratch_shapes=[
@@ -331,14 +399,16 @@
             pltpu.VMEM((2, 3, 8, cols, half), BF16),
             pltpu.VMEM((8, proj, seq), BF16),
             pltpu.VMEM((8, proj, seq), BF16),
+            pltpu.VMEM((proj, seq), F32),
+            pltpu.VMEM((proj, seq), F32),
             pltpu.VMEM((8, proj, seq), BF16),
             pltpu.VMEM((8, proj, seq), BF16),
-            pltpu.VMEM((2 * proj, seq), F32),
-            pltpu.VMEM((4, 16, 128), F32),
-            pltpu.VMEM((4, 16, 128), F32),
+            pltpu.VMEM((2, 2 * proj, seq), F32),
+            pltpu.VMEM((4, 8, 128), F32),
+            pltpu.VMEM((4, 8, 128), F32),
             dma((22,)), dma((2, 3, 2)), dma((2, 3, 2)), dma((2, 4, 4)), dma((2, 4)),
             dma((2, 3, 8)), dma((2, 3, 8)),
-            dma((8,)), dma((8,)), dma((2, 8)), dma((8,)), dma((4,)), dma((4,)),
+            dma((8,)), dma((8,)), dma, dma, dma((2, 8)), dma((8,)), dma((4,)), dma((4,)),
         ],
         compiler_params=pltpu.CompilerParams(
             collective_id=0, has_side_effects=True, vmem_limit_bytes=63 * 1024 * 1024
@@ -347,7 +417,7 @@
         g.reshape(tokens, local), acts.reshape(tokens, local), weights[0], down[0], up[0],
         wide_bits.T, rank_bits, lengths,
     )
-    return out[:, :, :proj].reshape(count, 1, 16 * proj)
+    return out.reshape(count, 1, 16 * proj)
 
 
 def solution(mesh):

time: 60 us -> 58.1 us (0.968)
  Pallas kernels: 58.3 us -> 56.6 us
    pallas_call x1, Pallas kernels: 58.3 us -> 56.6 us  [per_device(): pl.pallas_call(functools.partial(kernel, (local, proj, seq)), out_shape=j...]
    reshape x1 -> x0, local copies, waits for them, and re-layouts: 1.45 us -> none  [per_device(): return out[:, :, :proj].reshape(count, 1, 16 * proj)]
    unnamed x0 -> x1, local copies, waits for them, and re-layouts: none -> 1.32 us
where the time goes in v3:
time: 58.1 us; the launch traced here: 57.9 us
  Pallas kernels  56.6 us (97%)
  local copies, waits for them, and re-layouts  1.32 us (2%)
    pallas_call x1, Pallas kernels, per_device(): pl.pallas_call(functools.partial(kernel, (local, proj, seq)), out_shape=j...  56.6 us
    unnamed x1, local copies, waits for them, and re-layouts  1.32 us

profile of v3, /device:TPU:0, one launch (start us, length us, event | category | flops | bytes accessed | tf_op | source)
XLA Modules:
  0.0 57.9 jit_solution(357625935559179088)
XLA Ops:
  0.0 56.6 %shard_map.82 = f32[4,8,128]{2,1,0:T(8,128)} custom-call(bf16[512,1024]{1,0:T(8,128)(2,1)} %bitcast.10, bf16[512,1024]{1,0:T(8,128)(2,1)} %bitcast.11, bf16[1024,8192]{1,0:T(8,128)(2,1)} %bitcast.7, bf16[1024,128]{1,0:T(8,128)(2,1)} %bitcast.12, bf16[128,8192]{1,0:T(8,128)(2,1)} %bitcast.8, s32[64,8192]{1,0:T(8,128)} %bitcast.9, s32[128,128]{1,0:T(8,128)} %rank_hbm.1, ...), custom_call_target="tpu_custom_call" | custom-call | tf_op jit(solution)/shard_map/pallas_call | solution.py:380
  56.6 1.3 %copy.11 = f32[4,1,1024]{2,1,0:T(1,128)} copy(f32[4,1,1024]{2,1,0:T(1,128)} %bitcast.13) | data formatting | bytes 32768

commit v4 on v3

--- a/solution.py
+++ b/solution.py
@@ -42,8 +42,8 @@
     g_hbm, x_hbm, w_hbm, a_hbm, b_hbm, wide_hbm, rank_hbm, len_ref,
     out_ref,
     g_v, x_v, w_v, a_v, b_own, b_out, wide_v, rank_v, low_v,
-    vbuf, rt, gbuf, part, parts_in, x_out, x_in, x_sum, x_use, y_out, y_in, y_sum, f_out, f_in,
-    load_sem, rt_send, rt_recv, g_send, g_recv, p_send, p_recv,
+    vbuf, rt, gmid, gbuf, part, parts_in, x_out, x_in, x_sum, x_use, y_out, y_in, y_sum, f_out, f_in,
+    load_sem, rt_send, rt_recv, m_send, m_recv, g_send, g_recv, p_send, p_recv,
     x_send, x_recv, xs_send, xs_recv, y_send, y_recv, f_send, f_recv,
 ):
     local, proj, seq = sizes
@@ -80,8 +80,11 @@
         copy.start()
 
     barrier = pltpu.get_barrier_semaphore()
-    for i in range(1, 16):
-        there = {"pipe": (s + i // 4) % 4, "dp": (d + i % 4) % 4}
+    for i in range(1, 4):
+        pl.semaphore_signal(barrier, inc=1, device_id={"pipe": (s + i) % 4}, device_id_type=MESH)
+        pl.semaphore_signal(barrier, inc=1, device_id={"dp": (d + i) % 4}, device_id_type=MESH)
+    for i in (1, 3):
+        there = {"pipe": (s + i) % 4, "dp": zh * 2 + 1 - c}
         pl.semaphore_signal(barrier, inc=1, device_id=there, device_id_type=MESH)
     for i in range(1, 8):
         pl.semaphore_signal(barrier, inc=1, device_id={"tensor": (t + i) % 8}, device_id_type=MESH)
@@ -116,7 +119,7 @@
         gbuf[YP, 1] = p_t[:, half:]
 
     get_a.wait()
-    pl.semaphore_wait(barrier, 25)
+    pl.semaphore_wait(barrier, 18)
 
     def to_next(ch, k, core):
         return pltpu.make_async_remote_copy(
@@ -125,15 +128,24 @@
             device_id={"pipe": (s + 1) % 4, "dp": zh * 2 + core}, device_id_type=MESH,
         )
 
-    def to_final(ch, k, i):
-        return pltpu.make_async_remote_copy(
-            src_ref=vbuf.at[ch, k], dst_ref=gbuf.at[ch, c, my_cols],
-            send_sem=g_send.at[ch, k, i], recv_sem=g_recv.at[ch, d],
-            device_id={"pipe": (0, 2, 1, 3)[k], "dp": (d + i) % 4}, device_id_type=MESH,
-        )
-
-    def final_order(k):
-        return (2, 1, 3) if k == 3 else (2, 1, 3, 0)
+    def to_home(ch, k):
+        return pltpu.make_async_remote_copy(
+            src_ref=vbuf.at[ch, k], dst_ref=gmid.at[ch],
+            send_sem=m_send.at[ch, k], recv_sem=m_recv.at[ch],
+            device_id={"pipe": (0, 2, 1)[k]}, device_id_type=MESH,
+        )
+
+    def to_group(ch, i):
+        return pltpu.make_async_remote_copy(
+            src_ref=gmid.at[ch], dst_ref=gbuf.at[ch, c, my_cols],
+            send_sem=g_send.at[ch, i], recv_sem=g_recv.at[ch, d],
+            device_id={"dp": (d + i) % 4}, device_id_type=MESH,
+        )
+
+    def to_groups(ch):
+        gbuf[ch, c, my_cols] = gmid[ch]
+        for i in (2, 1, 3):
+            to_group(ch, i).start()
 
     def hand_on(ch, k):
         if k < 3:
@@ -141,13 +153,13 @@
             def _():
                 for core in range(2):
                     to_next(ch, k, core).start()
-        if ch == UQ or k > 0:
+        if k == 3:
+            gmid[ch] = vbuf[ch, k]
+            to_groups(ch)
+        elif ch == UQ or k > 0:
             @pl.when(s == 3)
             def _():
-                if k == 3:
-                    gbuf[ch, c, my_cols] = vbuf[ch, k]
-                for i in final_order(k):
-                    to_final(ch, k, i).start()
+                to_home(ch, k).start()
 
     def swap(out, into, send, recv, j):
         to = peer(j, 1)
@@ -275,22 +287,27 @@
 
     get_g.wait()
     for ch in (YP, UQ):
-        def arrived(src, ch=ch):
-            place = gbuf.at[ch, src % 2, pl.ds(pl.multiple_of((src // 2) * cols, cols), cols)]
+        first = 1 if ch == YP else 0
+
+        @pl.when((s < 3) & (s >= first))
+        def _(ch=ch):
             pltpu.make_async_remote_copy(
-                src_ref=vbuf.at[ch, 0], dst_ref=place,
-                send_sem=g_send.at[ch, 0, 0], recv_sem=g_recv.at[ch, src],
+                src_ref=vbuf.at[ch, 0], dst_ref=gmid.at[ch],
+                send_sem=m_send.at[ch, 0], recv_sem=m_recv.at[ch],
                 device_id={"pipe": (s + 1) % 4}, device_id_type=MESH,
             ).wait_recv()
-
-        @pl.when((s < 3) & (s >= (1 if ch == YP else 0)))
-        def _():
-            arrived(d)
-
-        @pl.when(s >= (1 if ch == YP else 0))
-        def _():
-            for i in range(1, 4):
-                arrived((d + i) % 4)
+            to_groups(ch)
+
+        @pl.when(s >= first)
+        def _(ch=ch):
+            for i in (1, 3, 2):
+                src = (d + i) % 4
+                place = gbuf.at[ch, src % 2, pl.ds(pl.multiple_of((src // 2) * cols, cols), cols)]
+                pltpu.make_async_remote_copy(
+                    src_ref=gmid.at[ch], dst_ref=place,
+                    send_sem=g_send.at[ch, 0], recv_sem=g_recv.at[ch, src],
+                    device_id={"dp": src}, device_id_type=MESH,
+                ).wait_recv()
 
         ys = nt(gbuf[ch, 0], g_v[:, :half]) + nt(gbuf[ch, 1], g_v[:, half:])
         ys = ys.astype(BF16)
@@ -344,9 +361,13 @@
 
         @pl.when(s == 3)
         def _(ch=ch):
-            for k in range(1 if ch == YP else 0, 4):
-                for i in final_order(k):
-                    to_final(ch, k, i).wait_send()
+            for k in range(1 if ch == YP else 0, 3):
+                to_home(ch, k).wait_send()
+
+        @pl.when(s >= (1 if ch == YP else 0))
+        def _(ch=ch):
+            for i in (2, 1, 3):
+                to_group(ch, i).wait_send()
 
         for k in range(1, 4):
             @pl.when(s >= k)
@@ -379,7 +400,7 @@
     hbm = pl.BlockSpec(memory_space=pltpu.HBM)
     out = pl.pallas_call(
         functools.partial(kernel, (local, proj, seq)),
-        out_shape=jax.ShapeDtypeStruct((count, 8, 128), F32),
+        out_shape=pltpu.VMEM((count, 8, 128), F32),
         in_specs=[hbm] * 7 + [pl.BlockSpec(memory_space=pltpu.SMEM)],
         out_specs=pl.BlockSpec(memory_space=pltpu.VMEM),
         scratch_shapes=[
@@ -394,6 +415,7 @@
             pltpu.VMEM((rank, 2 * proj), BF16),
             pltpu.VMEM((2, 4, cols, half), BF16),
             pltpu.VMEM((2, 3, 2, cols, half), BF16),
+            pltpu.VMEM((2, cols, half), BF16),
             pltpu.VMEM((2, 2, proj, half), BF16),
             pltpu.VMEM((2, 3, 8, cols, half), BF16),
             pltpu.VMEM((2, 3, 8, cols, half), BF16),
@@ -406,7 +428,7 @@
             pltpu.VMEM((2, 2 * proj, seq), F32),
             pltpu.VMEM((4, 8, 128), F32),
             pltpu.VMEM((4, 8, 128), F32),
-            dma((22,)), dma((2, 3, 2)), dma((2, 3, 2)), dma((2, 4, 4)), dma((2, 4)),
+            dma((22,)), dma((2, 3, 2)), dma((2, 3, 2)), dma((2, 3)), dma((2,)), dma((2, 4)), dma((2, 4)),
             dma((2, 3, 8)), dma((2, 3, 8)),
             dma((8,)), dma((8,)), dma, dma, dma((2, 8)), dma((8,)), dma((4,)), dma((4,)),
         ],

time: 58.1 us -> 54.9 us (0.945)
  Pallas kernels: 56.6 us -> 54.2 us
  local copies, waits for them, and re-layouts: 1.32 us -> 0.61 us
    pallas_call x1, Pallas kernels: 56.6 us -> 54.2 us  [per_device(): pl.pallas_call(functools.partial(kernel, (local, proj, seq)), out_shape=p...]
    unnamed x1, local copies, waits for them, and re-layouts: 1.32 us -> 0.61 us
where the time goes in v4:
time: 54.9 us; the launch traced here: 54.8 us
  Pallas kernels  54.2 us (99%)
  local copies, waits for them, and re-layouts  0.61 us (1%)
    pallas_call x1, Pallas kernels, per_device(): pl.pallas_call(functools.partial(kernel, (local, proj, seq)), out_shape=p...  54.2 us

profile of v4, /device:TPU:0, one launch (start us, length us, event | category | flops | bytes accessed | tf_op | source)
XLA Modules:
  0.0 54.8 jit_solution(13470660788736944697)
XLA Ops:
  0.0 54.2 %shard_map.82 = f32[4,8,128]{2,1,0:T(8,128)S(1)} custom-call(bf16[512,1024]{1,0:T(8,128)(2,1)} %bitcast.11, bf16[512,1024]{1,0:T(8,128)(2,1)} %bitcast.12, bf16[1024,8192]{1,0:T(8,128)(2,1)} %bitcast.8, bf16[1024,128]{1,0:T(8,128)(2,1)} %bitcast.13, bf16[128,8192]{1,0:T(8,128)(2,1)} %bitcast.9, s32[64,8192]{1,0:T(8,128)} %bitcast.10, s32[128,128]{1,0:T(8,128)} %rank_hbm.1, ...), custom_call_target="tpu_custom_call" | custom-call | tf_op jit(solution)/shard_map/pallas_call | solution.py:401
  54.2 0.6 %copy.11 = f32[4,1,1024]{2,1,0:T(1,128)} copy(f32[4,1,1024]{2,1,0:T(1,128)S(1)} %bitcast.7) | data formatting | bytes 32768

commit v5 on v4

--- a/solution.py
+++ b/solution.py
@@ -12,7 +12,8 @@
 F32 = jnp.float32
 BF16 = jnp.bfloat16
 MESH = pl.DeviceIdType.MESH
-SELF = 5
+ORDER = ((2, 1), (2, 0), (1, 1), (3, 1), (1, 0), (3, 0), (0, 1), (0, 0))
+SELF = 7
 YP, UQ = 0, 1
 
 
@@ -42,9 +43,9 @@
     g_hbm, x_hbm, w_hbm, a_hbm, b_hbm, wide_hbm, rank_hbm, len_ref,
     out_ref,
     g_v, x_v, w_v, a_v, b_own, b_out, wide_v, rank_v, low_v,
-    vbuf, rt, gmid, gbuf, part, parts_in, x_out, x_in, x_sum, x_use, y_out, y_in, y_sum, f_out, f_in,
+    vbuf, rt, gmid, gbuf, part, parts_in, x_out, x_in, x_sum, x_all, h_v, f_out, f_in,
     load_sem, rt_send, rt_recv, m_send, m_recv, g_send, g_recv, p_send, p_recv,
-    x_send, x_recv, xs_send, xs_recv, y_send, y_recv, f_send, f_recv,
+    x_send, x_recv, xs_send, xs_recv, f_send, f_recv,
 ):
     local, proj, seq = sizes
     half, cols = local // 2, proj // 2
@@ -57,7 +58,7 @@
     home = s + edge * (3 - 2 * s)
 
     def peer(j, sign):
-        dx, dz = (j // 2 + 2) % 4, 1 - j % 2
+        dx, dz = ORDER[j]
         return ((z + dz) % 2) * 4 + (x + sign * dx + 4) % 4
 
     def load(src, dst, i):
@@ -88,9 +89,12 @@
         pl.semaphore_signal(barrier, inc=1, device_id=there, device_id_type=MESH)
     for i in range(1, 8):
         pl.semaphore_signal(barrier, inc=1, device_id={"tensor": (t + i) % 8}, device_id_type=MESH)
-    for i in range(1, 4):
-        there = {"pipe": 3 - s, "tensor": z * 4 + (x + i) % 4}
-        pl.semaphore_signal(barrier, inc=1, device_id=there, device_id_type=MESH)
+
+    @pl.when(edge == 1)
+    def _():
+        for i in range(1, 8):
+            there = {"pipe": home, "tensor": (t + i) % 8}
+            pl.semaphore_signal(barrier, inc=1, device_id=there, device_id_type=MESH)
 
     @pl.when(s >= 1)
     def _():
@@ -119,7 +123,7 @@
         gbuf[YP, 1] = p_t[:, half:]
 
     get_a.wait()
-    pl.semaphore_wait(barrier, 18)
+    pl.semaphore_wait(barrier, 15 + 7 * edge)
 
     def to_next(ch, k, core):
         return pltpu.make_async_remote_copy(
@@ -194,21 +198,50 @@
             if j != SELF:
                 swap(x_out, x_in, x_send, x_recv, j).start()
 
-    x_cross = pltpu.make_async_remote_copy(
-        src_ref=x_sum, dst_ref=x_use, send_sem=xs_send, recv_sem=xs_recv,
-        device_id={"pipe": home}, device_id_type=MESH,
-    )
+    def share_x(i):
+        return pltpu.make_async_remote_copy(
+            src_ref=x_sum, dst_ref=x_all.at[t], send_sem=xs_send.at[i], recv_sem=xs_recv.at[t],
+            device_id={"pipe": home, "tensor": (t + i) % 8}, device_id_type=MESH,
+        )
 
     def sum_x():
-        x_sum[...] = total(x_out, x_in, x_send, x_recv)
+        x_sum[...] = total(x_out, x_in, x_send, x_recv).astype(BF16)
+        for i in range(1, 8):
+            share_x(i).start()
 
         @pl.when(edge == 1)
         def _():
-            x_cross.start()
+            share_x(0).start()
 
         @pl.when(edge == 0)
         def _():
-            x_use[...] = x_sum[...]
+            x_all[t] = x_sum[...]
+
+    def make_h():
+        def arrived(i):
+            src = (t + i) % 8
+            pltpu.make_async_remote_copy(
+                src_ref=x_sum, dst_ref=x_all.at[src], send_sem=xs_send.at[i], recv_sem=xs_recv.at[src],
+                device_id={"pipe": home, "tensor": (t + 1) % 8}, device_id_type=MESH,
+            ).wait_recv()
+
+        for i in range(1, 8):
+            arrived(i)
+
+        @pl.when(edge == 1)
+        def _():
+            arrived(0)
+
+        get_g.wait()
+        token = lax.broadcasted_iota(jnp.int32, (proj, seq), 1)
+        for e in range(4):
+            given = g_v[e * seq : (e + 1) * seq]
+            for ch in (YP, UQ):
+                xt = x_all[(1 - ch) * 4 + e].astype(F32)
+                xt = jnp.where(token < len_ref[e], xt, 0.0).astype(BF16)
+                h = dot(xt, given).astype(BF16)
+                for q in range(2):
+                    h_v[ch, q, e * cols : (e + 1) * cols] = h[q * cols : (q + 1) * cols]
 
     @pl.when(s == 0)
     def _():
@@ -254,38 +287,32 @@
                     project_x()
                 if ch == YP and k == 2:
                     sum_x()
-
-    def y_swap(ch, i):
-        e = (x + i) % 4
-        to = (1 - ch) * 4 + e
-        return pltpu.make_async_remote_copy(
-            src_ref=y_out.at[to], dst_ref=y_in.at[t], send_sem=y_send.at[ch, i], recv_sem=y_recv.at[t],
-            device_id={"tensor": to}, device_id_type=MESH,
-        )
-
-    def y_each(ch, act):
+                if ch == YP and k == 3:
+                    make_h()
+
+    @pl.when(s == 1)
+    def _():
+        sum_x()
+
+    @pl.when(s < 3)
+    def _():
+        make_h()
+
+    def f_swap(ch, i):
+        to = (x + i) % 4
+        return pltpu.make_async_remote_copy(
+            src_ref=f_out.at[ch, to], dst_ref=f_in.at[t], send_sem=f_send.at[ch, i], recv_sem=f_recv.at[t],
+            device_id={"pipe": home, "tensor": (1 - ch) * 4 + to}, device_id_type=MESH,
+        )
+
+    def f_each(ch, act):
         for i in (2, 1, 3):
-            act(y_swap(ch, i))
-
-        @pl.when(z == ch)
+            act(f_swap(ch, i))
+
+        @pl.when((edge == 1) | (z == ch))
         def _():
-            act(y_swap(ch, 0))
-
-    @pl.when(s == 1)
-    def _():
-        sum_x()
-
-    @pl.when(edge == 1)
-    def _():
-        x_cross.wait_recv()
-
-    xt = x_use[...]
-    token = lax.broadcasted_iota(jnp.int32, xt.shape, 1)
-    scale = ADAPTER_SCALE / math.sqrt(seq) / math.sqrt(local * 8) / math.sqrt(128)
-    xt = jnp.where(token < len_ref[x], xt * scale, 0.0)
-    y_sum[...] = jnp.zeros_like(y_sum)
-
-    get_g.wait()
+            act(f_swap(ch, 0))
+
     for ch in (YP, UQ):
         first = 1 if ch == YP else 0
 
@@ -309,48 +336,37 @@
                     device_id={"dp": src}, device_id_type=MESH,
                 ).wait_recv()
 
-        ys = nt(gbuf[ch, 0], g_v[:, :half]) + nt(gbuf[ch, 1], g_v[:, half:])
-        ys = ys.astype(BF16)
+        halves = [
+            nt(h_v[ch, q, :, :half], gbuf[ch, 0]) + nt(h_v[ch, q, :, half:], gbuf[ch, 1]) for q in range(2)
+        ]
+        full = jnp.concatenate(halves, axis=1)
         for e in range(4):
-            y_out[(1 - ch) * 4 + e] = ys[:, e * seq : (e + 1) * seq]
-        y_each(ch, lambda copy: copy.start())
-
-    yt = total(y_out, y_in, y_send.at[0], y_recv)
-    y_sum[0, :proj] = yt
-    y_sum[1, proj:] = yt
-    exact = lax.Precision.HIGHEST
-    full = nt(xt[:cols], y_sum[0], precision=exact) + nt(xt[cols:], y_sum[1], precision=exact)
-    f_out[...] = full.reshape(f_out.shape)
-
-    def f_swap(i):
-        to = (x + i) % 4
-        return pltpu.make_async_remote_copy(
-            src_ref=f_out.at[to], dst_ref=f_in.at[x], send_sem=f_send.at[i], recv_sem=f_recv.at[x],
-            device_id={"pipe": home, "tensor": z * 4 + to}, device_id_type=MESH,
-        )
-
-    def f_arrived(i):
-        src = (x + i) % 4
+            for p in range(4):
+                at = e * cols + p * 8
+                f_out[ch, p, e] = full[at : at + 8]
+        f_each(ch, lambda copy: copy.start())
+
+    def f_arrived(j):
+        src = peer(j, -1)
         pltpu.make_async_remote_copy(
-            src_ref=f_out.at[0], dst_ref=f_in.at[src], send_sem=f_send.at[i], recv_sem=f_recv.at[src],
-            device_id={"pipe": home, "tensor": z * 4 + (x + 1) % 4}, device_id_type=MESH,
+            src_ref=f_out.at[0, 0], dst_ref=f_in.at[src], send_sem=f_send.at[0, 0], recv_sem=f_recv.at[src],
+            device_id={"pipe": home, "tensor": (t + 1) % 8}, device_id_type=MESH,
         ).wait_recv()
-
-    for i in (2, 1, 3):
-        f_swap(i).start()
+        return f_in[src]
 
     @pl.when(edge == 1)
     def _():
-        f_swap(0).start()
-        f_arrived(0)
+        f_arrived(SELF)
 
     @pl.when(edge == 0)
     def _():
-        f_in[x] = f_out[x]
-
-    for i in (1, 3, 2):
-        f_arrived(i)
-    out_ref[...] = f_in[...]
+        f_in[t] = f_out[1 - z, x]
+
+    acc = f_in[t]
+    for j in reversed(range(7)):
+        acc = acc + f_arrived(j)
+    scale = ADAPTER_SCALE / math.sqrt(seq) / math.sqrt(local * 8) / math.sqrt(128)
+    out_ref[...] = acc * scale
 
     for ch in (YP, UQ):
         for k in range(1 if ch == YP else 0, 3):
@@ -376,18 +392,17 @@
                     if j != SELF:
                         swap(*group(ch, k), j).wait_send()
 
-        y_each(ch, lambda copy: copy.wait_send())
+        f_each(ch, lambda copy: copy.wait_send())
 
     for j in range(8):
         if j != SELF:
             swap(x_out, x_in, x_send, x_recv, j).wait_send()
-    for i in (2, 1, 3):
-        f_swap(i).wait_send()
+    for i in range(1, 8):
+        share_x(i).wait_send()
 
     @pl.when(edge == 1)
     def _():
-        f_swap(0).wait_send()
-        x_cross.wait_send()
+        share_x(0).wait_send()
 
 
 def per_device(g, acts, weights, down, up, wide_bits, rank_bits, lengths):
@@ -421,16 +436,14 @@
             pltpu.VMEM((2, 3, 8, cols, half), BF16),
             pltpu.VMEM((8, proj, seq), BF16),
             pltpu.VMEM((8, proj, seq), BF16),
-            pltpu.VMEM((proj, seq), F32),
-            pltpu.VMEM((proj, seq), F32),
+            pltpu.VMEM((proj, seq), BF16),
             pltpu.VMEM((8, proj, seq), BF16),
-            pltpu.VMEM((8, proj, seq), BF16),
-            pltpu.VMEM((2, 2 * proj, seq), F32),
-            pltpu.VMEM((4, 8, 128), F32),
-            pltpu.VMEM((4, 8, 128), F32),
+            pltpu.VMEM((2, 2, 4 * cols, local), BF16),
+            pltpu.VMEM((2, 4, 4, 8, 128), F32),
+            pltpu.VMEM((8, 4, 8, 128), F32),
             dma((22,)), dma((2, 3, 2)), dma((2, 3, 2)), dma((2, 3)), dma((2,)), dma((2, 4)), dma((2, 4)),
             dma((2, 3, 8)), dma((2, 3, 8)),
-            dma((8,)), dma((8,)), dma, dma, dma((2, 8)), dma((8,)), dma((4,)), dma((4,)),
+            dma((8,)), dma((8,)), dma((8,)), dma((8,)), dma((2, 4)), dma((8,)),
         ],
         compiler_params=pltpu.CompilerParams(
             collective_id=0, has_side_effects=True, vmem_limit_bytes=63 * 1024 * 1024

time: 54.9 us -> 52.7 us (0.960)
  Pallas kernels: 54.2 us -> 51.6 us
    pallas_call x1, Pallas kernels: 54.2 us -> 51.6 us  [per_device(): pl.pallas_call(functools.partial(kernel, (local, proj, seq)), out_shape=p...]
where the time goes in v5:
time: 52.7 us; the launch traced here: 52.2 us
  Pallas kernels  51.6 us (98%)
  local copies, waits for them, and re-layouts  0.61 us (1%)
    pallas_call x1, Pallas kernels, per_device(): pl.pallas_call(functools.partial(kernel, (local, proj, seq)), out_shape=p...  51.6 us

profile of v5, /device:TPU:0, one launch (start us, length us, event | category | flops | bytes accessed | tf_op | source)
XLA Modules:
  0.0 52.2 jit_solution(10197105972745112886)
XLA Ops:
  0.0 51.6 %shard_map.82 = f32[4,8,128]{2,1,0:T(8,128)S(1)} custom-call(bf16[512,1024]{1,0:T(8,128)(2,1)} %bitcast.11, bf16[512,1024]{1,0:T(8,128)(2,1)} %bitcast.12, bf16[1024,8192]{1,0:T(8,128)(2,1)} %bitcast.8, bf16[1024,128]{1,0:T(8,128)(2,1)} %bitcast.13, bf16[128,8192]{1,0:T(8,128)(2,1)} %bitcast.9, s32[64,8192]{1,0:T(8,128)} %bitcast.10, s32[128,128]{1,0:T(8,128)} %rank_hbm.1, ...), custom_call_target="tpu_custom_call" | custom-call | tf_op jit(solution)/shard_map/pallas_call | solution.py:416
  51.6 0.6 %copy.11 = f32[4,1,1024]{2,1,0:T(1,128)} copy(f32[4,1,1024]{2,1,0:T(1,128)S(1)} %bitcast.7) | data formatting | bytes 32768

commit v6 on v5

--- a/solution.py
+++ b/solution.py
@@ -75,10 +75,27 @@
     get_a = load(a_hbm, a_v, 3)
     get_x = load(x_hbm, x_v, 4)
     get_g = load(g_hbm, g_v, 5)
-    get_b = [load(b_hbm.at[:, cols_of(u)], b_out.at[u], 6 + u) for u in range(8)]
-    get_w = [load(w_hbm.at[:, cols_of(u)], w_v.at[u], 14 + u) for u in range(8)]
-    for copy in (get_rank, get_own, get_wide, get_a, get_x):
+
+    def weights_of(j):
+        u = peer(j, 1)
+        return (
+            load(b_hbm.at[:, cols_of(u)], b_out.at[u], 6 + j),
+            load(w_hbm.at[:, cols_of(u)], w_v.at[u], 14 + j),
+        )
+
+    for copy in (get_rank, get_own, get_wide, get_a):
         copy.start()
+
+    @pl.when(s >= 1)
+    def _():
+        for j in range(8):
+            for copy in weights_of(j):
+                copy.start()
+
+    @pl.when(s == 0)
+    def _():
+        get_x.start()
+        get_g.start()
 
     barrier = pltpu.get_barrier_semaphore()
     for i in range(1, 4):
@@ -90,18 +107,9 @@
     for i in range(1, 8):
         pl.semaphore_signal(barrier, inc=1, device_id={"tensor": (t + i) % 8}, device_id_type=MESH)
 
-    @pl.when(edge == 1)
-    def _():
-        for i in range(1, 8):
-            there = {"pipe": home, "tensor": (t + i) % 8}
-            pl.semaphore_signal(barrier, inc=1, device_id=there, device_id_type=MESH)
-
-    @pl.when(s >= 1)
-    def _():
-        for copy in get_w + get_b:
-            copy.start()
-
-    get_g.start()
+    for i in range(1, 8):
+        there = {"pipe": 3 - s, "tensor": (t + i) % 8}
+        pl.semaphore_signal(barrier, inc=1, device_id=there, device_id_type=MESH)
 
     get_rank.wait()
     low_v[...] = nt(reorder(128, proj), signs_of(rank_v[...])).astype(BF16)
@@ -123,7 +131,7 @@
         gbuf[YP, 1] = p_t[:, half:]
 
     get_a.wait()
-    pl.semaphore_wait(barrier, 15 + 7 * edge)
+    pl.semaphore_wait(barrier, 22)
 
     def to_next(ch, k, core):
         return pltpu.make_async_remote_copy(
@@ -267,6 +275,9 @@
 
         for j in range(8):
             to = peer(j, 1)
+            if ch == YP and k == 1:
+                for copy in weights_of(j):
+                    copy.wait()
             value = dot(r0, w_v[to, :half]) + dot(r1, w_v[to, half:]) + dot(small, b_out[to])
             part[ch, i, to] = value.astype(BF16)
             if j != SELF:
@@ -275,11 +286,11 @@
     for k in range(1, 4):
         @pl.when(s >= k)
         def _(k=k):
+            multiply(YP, k)
             if k == 1:
-                for copy in get_w + get_b:
-                    copy.wait()
-            for ch in (YP, UQ):
-                multiply(ch, k)
+                get_x.start()
+                get_g.start()
+            multiply(UQ, k)
             for ch in (YP, UQ):
                 vbuf[ch, k] = total(*group(ch, k)).astype(BF16)
                 hand_on(ch, k)
@@ -287,8 +298,10 @@
                     project_x()
                 if ch == YP and k == 2:
                     sum_x()
-                if ch == YP and k == 3:
-                    make_h()
+
+                    @pl.when(s == 3)
+                    def _():
+                        make_h()
 
     @pl.when(s == 1)
     def _():

time: 52.7 us -> 52.6 us (level)
  no operation moved by 1% of the time
where the time goes in v6:
time: 52.6 us; the launch traced here: 52.4 us
  Pallas kernels  51.8 us (98%)
  local copies, waits for them, and re-layouts  0.61 us (1%)
    pallas_call x1, Pallas kernels, per_device(): pl.pallas_call(functools.partial(kernel, (local, proj, seq)), out_shape=p...  51.8 us

profile of v6, /device:TPU:0, one launch (start us, length us, event | category | flops | bytes accessed | tf_op | source)
XLA Modules:
  0.0 52.4 jit_solution(14686259953169587680)
XLA Ops:
  0.0 51.8 %shard_map.82 = f32[4,8,128]{2,1,0:T(8,128)S(1)} custom-call(bf16[512,1024]{1,0:T(8,128)(2,1)} %bitcast.11, bf16[512,1024]{1,0:T(8,128)(2,1)} %bitcast.12, bf16[1024,8192]{1,0:T(8,128)(2,1)} %bitcast.8, bf16[1024,128]{1,0:T(8,128)(2,1)} %bitcast.13, bf16[128,8192]{1,0:T(8,128)(2,1)} %bitcast.9, s32[64,8192]{1,0:T(8,128)} %bitcast.10, s32[128,128]{1,0:T(8,128)} %rank_hbm.1, ...), custom_call_target="tpu_custom_call" | custom-call | tf_op jit(solution)/shard_map/pallas_call | solution.py:429
  51.8 0.6 %copy.11 = f32[4,1,1024]{2,1,0:T(1,128)} copy(f32[4,1,1024]{2,1,0:T(1,128)S(1)} %bitcast.7) | data formatting | bytes 32768

commit v7 on v6

--- a/solution.py
+++ b/solution.py
@@ -12,7 +12,7 @@
 F32 = jnp.float32
 BF16 = jnp.bfloat16
 MESH = pl.DeviceIdType.MESH
-ORDER = ((2, 1), (2, 0), (1, 1), (3, 1), (1, 0), (3, 0), (0, 1), (0, 0))
+ORDER = ((2, 1), (1, 1), (3, 1), (2, 0), (0, 1), (1, 0), (3, 0), (0, 0))
 SELF = 7
 YP, UQ = 0, 1
 
@@ -42,7 +42,7 @@
     sizes,
     g_hbm, x_hbm, w_hbm, a_hbm, b_hbm, wide_hbm, rank_hbm, len_ref,
     out_ref,
-    g_v, x_v, w_v, a_v, b_own, b_out, wide_v, rank_v, low_v,
+    g_v, x_v, w_v, a_v, b_own, wide_v, rank_v, low_v,
     vbuf, rt, gmid, gbuf, part, parts_in, x_out, x_in, x_sum, x_all, h_v, f_out, f_in,
     load_sem, rt_send, rt_recv, m_send, m_recv, g_send, g_recv, p_send, p_recv,
     x_send, x_recv, xs_send, xs_recv, f_send, f_recv,
@@ -79,8 +79,8 @@
     def weights_of(j):
         u = peer(j, 1)
         return (
-            load(b_hbm.at[:, cols_of(u)], b_out.at[u], 6 + j),
-            load(w_hbm.at[:, cols_of(u)], w_v.at[u], 14 + j),
+            load(b_hbm.at[:, cols_of(u)], w_v.at[u, local:], 6 + j),
+            load(w_hbm.at[:, cols_of(u)], w_v.at[u, :local], 14 + j),
         )
 
     for copy in (get_rank, get_own, get_wide, get_a):
@@ -272,14 +272,14 @@
         r0, r1 = rt[ch, i, 0], rt[ch, i, 1]
         small = dot(r0, a_v[:half]) + dot(r1, a_v[half:])
         small = (ADAPTER_SCALE * small).astype(BF16)
+        whole = jnp.concatenate([r0, r1, small], axis=1)
 
         for j in range(8):
             to = peer(j, 1)
             if ch == YP and k == 1:
                 for copy in weights_of(j):
                     copy.wait()
-            value = dot(r0, w_v[to, :half]) + dot(r1, w_v[to, half:]) + dot(small, b_out[to])
-            part[ch, i, to] = value.astype(BF16)
+            part[ch, i, to] = dot(whole, w_v[to]).astype(BF16)
             if j != SELF:
                 swap(*group(ch, k), j).start()
 
@@ -434,10 +434,9 @@
         scratch_shapes=[
             pltpu.VMEM((tokens, local), BF16),
             pltpu.VMEM((tokens, local), BF16),
-            pltpu.VMEM((8, local, half), BF16),
+            pltpu.VMEM((8, local + rank, half), BF16),
             pltpu.VMEM((local, rank), BF16),
             pltpu.VMEM((rank, local), BF16),
-            pltpu.VMEM((8, rank, half), BF16),
             pltpu.VMEM((proj, local), jnp.int32),
             pltpu.VMEM((rank, 2 * proj), jnp.int32),
             pltpu.VMEM((rank, 2 * proj), BF16),

time: 52.6 us -> 51.3 us (0.975)
  Pallas kernels: 51.8 us -> 50.3 us
    pallas_call x1, Pallas kernels: 51.8 us -> 50.3 us  [per_device(): pl.pallas_call(functools.partial(kernel, (local, proj, seq)), out_shape=p...]
where the time goes in v7:
time: 51.3 us; the launch traced here: 51 us
  Pallas kernels  50.3 us (98%)
  local copies, waits for them, and re-layouts  0.61 us (1%)
    pallas_call x1, Pallas kernels, per_device(): pl.pallas_call(functools.partial(kernel, (local, proj, seq)), out_shape=p...  50.3 us

profile of v7, /device:TPU:0, one launch (start us, length us, event | category | flops | bytes accessed | tf_op | source)
XLA Modules:
  0.0 51.0 jit_solution(8980952863668518149)
XLA Ops:
  0.0 50.3 %shard_map.82 = f32[4,8,128]{2,1,0:T(8,128)S(1)} custom-call(bf16[512,1024]{1,0:T(8,128)(2,1)} %bitcast.11, bf16[512,1024]{1,0:T(8,128)(2,1)} %bitcast.12, bf16[1024,8192]{1,0:T(8,128)(2,1)} %bitcast.8, bf16[1024,128]{1,0:T(8,128)(2,1)} %bitcast.13, bf16[128,8192]{1,0:T(8,128)(2,1)} %bitcast.9, s32[64,8192]{1,0:T(8,128)} %bitcast.10, s32[128,128]{1,0:T(8,128)} %rank_hbm.1, ...), custom_call_target="tpu_custom_call" | custom-call | tf_op jit(solution)/shard_map/pallas_call | solution.py:429
  50.3 0.6 %copy.11 = f32[4,1,1024]{2,1,0:T(1,128)} copy(f32[4,1,1024]{2,1,0:T(1,128)S(1)} %bitcast.7) | data formatting | bytes 32768

commit v8 on v7

--- a/solution.py
+++ b/solution.py
@@ -12,7 +12,7 @@
 F32 = jnp.float32
 BF16 = jnp.bfloat16
 MESH = pl.DeviceIdType.MESH
-ORDER = ((2, 1), (1, 1), (3, 1), (2, 0), (0, 1), (1, 0), (3, 0), (0, 0))
+ORDER = ((2, 1), (1, 1), (3, 1), (0, 1), (2, 0), (1, 0), (3, 0), (0, 0))
 SELF = 7
 YP, UQ = 0, 1
 

time: 51.3 us -> 50.6 us (0.986)
  Pallas kernels: 50.3 us -> 49.7 us
    pallas_call x1, Pallas kernels: 50.3 us -> 49.7 us  [per_device(): pl.pallas_call(functools.partial(kernel, (local, proj, seq)), out_shape=p...]
where the time goes in v8:
time: 50.6 us; the launch traced here: 50.3 us
  Pallas kernels  49.7 us (98%)
  local copies, waits for them, and re-layouts  0.61 us (1%)
    pallas_call x1, Pallas kernels, per_device(): pl.pallas_call(functools.partial(kernel, (local, proj, seq)), out_shape=p...  49.7 us

profile of v8, /device:TPU:0, one launch (start us, length us, event | category | flops | bytes accessed | tf_op | source)
XLA Modules:
  0.0 50.3 jit_solution(17951660888637363141)
XLA Ops:
  0.0 49.7 %shard_map.82 = f32[4,8,128]{2,1,0:T(8,128)S(1)} custom-call(bf16[512,1024]{1,0:T(8,128)(2,1)} %bitcast.11, bf16[512,1024]{1,0:T(8,128)(2,1)} %bitcast.12, bf16[1024,8192]{1,0:T(8,128)(2,1)} %bitcast.8, bf16[1024,128]{1,0:T(8,128)(2,1)} %bitcast.13, bf16[128,8192]{1,0:T(8,128)(2,1)} %bitcast.9, s32[64,8192]{1,0:T(8,128)} %bitcast.10, s32[128,128]{1,0:T(8,128)} %rank_hbm.1, ...), custom_call_target="tpu_custom_call" | custom-call | tf_op jit(solution)/shard_map/pallas_call | solution.py:429
  49.7 0.6 %copy.11 = f32[4,1,1024]{2,1,0:T(1,128)} copy(f32[4,1,1024]{2,1,0:T(1,128)S(1)} %bitcast.7) | data formatting | bytes 32768
